TPU v7x, 256 devices: a whole 4x4x8 slice. The times are simulated.
256 devices in a mesh: plane: 2 (over core), row: 8 (over z), col: 16 (over y, x).
Axes of the slice: x: 4, y: 4, z: 8, core: 2. Of those that a mesh axis runs over, the one named last changes fastest.
Arguments:
- velocity: float32 [3, 4, 4096, 4096], P(None, 'plane', 'row', 'col'), may hold values from -60 to 60
Outputs:
- dissipation: float32 [4, 4096, 4096], P('plane', 'row', 'col')
- fine_means: float32 [128, 128], P('row', 'col')
- coarse_means: float32 [4, 4], replicated
All inputs are finite; a program needn't handle non-finite values.
Results may differ from a plain program's by a relative error of at most 0.000078.
Values sent between devices are 32-bit elements; how exact they have to be, the bound alone decides.
No kernel may reach another device: no remote copies, remote signals or barrier semaphores. Data moves between devices by JAX's collectives and lax.ppermute only.
A program may use at most 128 MiB of HBM per device.

v0:
```python
import functools
import math

import jax
import jax.numpy as jnp
from jax import lax
from jax.sharding import Mesh
from jax.sharding import PartitionSpec as P

N = 4096
FIRST = 32
FINE = 32
COARSE = 1024
PLANE_COL = ("plane", "col_0", "col_1")
COL = ("col_0", "col_1")
ROW_COL = ("row", "col_0", "col_1")


precise = lax.Precision.HIGHEST


def split_up(shard, dim, size):
    lengths = shard.shape
    blocks = shard.reshape(*lengths[:dim], size, lengths[dim] // size, *lengths[dim + 1 :])
    return jnp.moveaxis(blocks, dim, 0)


def cut_rows(length, count):
    turn = length // count
    if turn >= 8:
        turn -= turn % 8
    return [turn * k for k in range(1, count)]


def in_order(blocks, dim):
    lengths = list(blocks.shape[1:])
    lengths[dim] *= blocks.shape[0]
    return jnp.moveaxis(blocks, 0, dim).reshape(lengths)


def exchange_in_pieces(shard, axis, pieces, split_dim, concat_dim):
    blocks = split_up(shard, split_dim, lax.axis_size(axis))
    widest = max(range(1, max(2, blocks.ndim - 1)), key=lambda d: blocks.shape[d])
    outs = []
    for share in jnp.split(blocks, cut_rows(blocks.shape[widest], pieces), axis=widest):
        if share.size:
            outs.append(lax.all_to_all(share, axis, split_axis=0, concat_axis=0, tiled=True))
    return in_order(jnp.concatenate(outs, axis=widest), concat_dim)


def exchange_both(shard, axis, axes, splits, concats):
    sizes = [lax.axis_size(a) for a in axes]
    blocks = split_up(shard, splits[0], sizes[0])
    blocks = jnp.moveaxis(split_up(blocks, splits[1] + 1, sizes[1]), 0, 1)
    inside = blocks.shape[2:]
    blocks = blocks.reshape(-1, *inside)
    blocks = lax.all_to_all(blocks, axis, split_axis=0, concat_axis=0, tiled=True)
    blocks = in_order(blocks.reshape(*sizes, *inside), concats[0] + 1)
    return in_order(blocks, concats[1])


def gathered_total(shard, axis):
    return lax.all_gather(shard, axis).sum(0)


def over_axes(shard, axes):
    return functools.reduce(lax.psum, axes, shard)


def angle_table(height, across, modulus):
    left_idx = lax.broadcasted_iota(jnp.int32, (height, across), 0)
    right_idx = lax.broadcasted_iota(jnp.int32, (height, across), 1)
    turn_count = left_idx * right_idx % modulus
    phase_ang = turn_count.astype(jnp.float32) * (2.0 * math.pi / modulus)
    return (jnp.cos(phase_ang), jnp.sin(phase_ang))


def wave_table(first_len, second, length):
    low_idx = lax.broadcasted_iota(jnp.int32, (first_len, second), 0)
    high_idx = lax.broadcasted_iota(jnp.int32, (first_len, second), 1)
    indices = low_idx + first_len * high_idx
    signed = jnp.where(indices < length // 2, indices, indices - length)
    signed = jnp.where(indices == length // 2, 0, signed)
    return signed.astype(jnp.float32) * (2.0 * math.pi / length)


def left_mult(coeffs, values):
    return jnp.einsum("kn,...nm->...km", coeffs, values, precision=precise)


def right_mult(values, coeffs):
    return jnp.einsum("...kn,nm->...km", values, coeffs, precision=precise)


def derivative_last(values):
    length = values.shape[-1]
    first_len = FIRST
    second = length // first_len
    leading = values.shape[:-1]
    blocks = values.reshape(leading + (first_len, second))
    cos_a, sin_a = angle_table(first_len, first_len, first_len)
    cos_b, sin_b = angle_table(second, second, second)
    cos_t, sin_t = angle_table(first_len, second, length)
    forward_a = jnp.concatenate([cos_a, -sin_a], axis=0)
    section_a = left_mult(forward_a, blocks)
    real_a = section_a[..., :first_len, :]
    imag_a = section_a[..., first_len:, :]
    real_b = real_a * cos_t + imag_a * sin_t
    imag_b = imag_a * cos_t - real_a * sin_t
    forward_b = jnp.concatenate(
        [jnp.concatenate([cos_b, -sin_b], axis=1), jnp.concatenate([sin_b, cos_b], axis=1)], axis=0
    )
    section_c = right_mult(jnp.concatenate([real_b, imag_b], axis=-1), forward_b)
    wavenum = wave_table(first_len, second, length)
    scaled = jnp.concatenate(
        [-wavenum * section_c[..., second:], wavenum * section_c[..., :second]], axis=-1
    )
    inverse_b = jnp.concatenate(
        [jnp.concatenate([cos_b, sin_b], axis=1), jnp.concatenate([-sin_b, cos_b], axis=1)], axis=0
    )
    section_e = right_mult(scaled, inverse_b)
    real_e = section_e[..., :second]
    imag_e = section_e[..., second:]
    real_f = real_e * cos_t - imag_e * sin_t
    imag_f = real_e * sin_t + imag_e * cos_t
    inverse_a = jnp.concatenate([cos_a, -sin_a], axis=1)
    result = left_mult(inverse_a, jnp.concatenate([real_f, imag_f], axis=-2)) * (1.0 / length)
    return result.reshape(leading + (length,))


def along_rows(pencil):
    turned = jnp.swapaxes(pencil, 2, 3)
    back_turned = jnp.swapaxes(derivative_last(turned), 2, 3)
    return exchange_in_pieces(back_turned, "row", 2, 2, 3)


def per_device(velocity):
    x_local = velocity.shape[2]
    y_local = velocity.shape[3]
    plane_count = velocity.shape[1] * lax.axis_size("plane")
    grad_x = along_rows(lax.all_to_all(velocity, "row", split_axis=3, concat_axis=2, tiled=True))
    slab_data = exchange_both(velocity, PLANE_COL, ("plane", COL), (2, 2), (1, 3))
    slab_y = derivative_last(slab_data)
    slab_z = (jnp.roll(slab_data, -1, axis=1) - jnp.roll(slab_data, 1, axis=1)) * 0.5
    cross_yz = slab_z[1] + slab_y[2]
    partial_value = slab_y[1] * slab_y[1] + slab_z[2] * slab_z[2] + 0.5 * cross_yz * cross_yz
    packed = jnp.stack([partial_value, slab_y[0], slab_z[0]])
    packed = lax.all_to_all(packed, COL, split_axis=3, concat_axis=2, tiled=True)
    packed = lax.all_to_all(packed, "plane", split_axis=1, concat_axis=2, tiled=True)
    cross_xy = packed[1] + grad_x[1]
    cross_xz = packed[2] + grad_x[2]
    dissip = packed[0] + grad_x[0] * grad_x[0]
    dissip = dissip + 0.5 * (cross_xy * cross_xy + cross_xz * cross_xz)
    column_sum = jnp.sum(dissip, axis=0)
    fine_local = column_sum.reshape(x_local // FINE, FINE, y_local // FINE, FINE).sum(axis=(1, 3))
    fine_total = gathered_total(fine_local, "plane")
    fine_means = fine_total * (1.0 / (plane_count * FINE * FINE))
    local_total = jnp.sum(fine_total)
    box_count = N // COARSE
    box_row = lax.axis_index("row") * x_local // COARSE
    box_col = lax.axis_index(COL) * y_local // COARSE
    rows_hit = (lax.iota(jnp.int32, box_count) == box_row).astype(jnp.float32)
    cols_hit = (lax.iota(jnp.int32, box_count) == box_col).astype(jnp.float32)
    partial_map = rows_hit[:, None] * cols_hit[None, :] * local_total
    coarse_total = over_axes(partial_map, ROW_COL)
    coarse_means = coarse_total * (1.0 / (plane_count * COARSE * COARSE))
    return (dissip, fine_means, coarse_means)


def solution(mesh):
    split = Mesh(
        mesh.devices.reshape(mesh.shape["plane"], mesh.shape["row"], 4, 4),
        ("plane", "row", "col_0", "col_1"),
    )
    in_specs = (P(None, "plane", "row", COL),)
    out_specs = (P("plane", "row", COL), P("row", COL), P())
    return jax.shard_map(
        per_device, mesh=split, in_specs=in_specs, out_specs=out_specs, check_vma=False
    )
```

profile of v0, /device:TPU:2, one launch (start us, length us, event | category | flops | bytes accessed | tf_op | source)
XLA Modules:
  0.0 436.9 jit_solution(4735583663950403906)
XLA Ops:
  0.6 4.0 copy.91
  4.6 7.9 %all-to-all-start = ((f32[32,3,2,16,256]{4,3,2,1,0:T(8,128)}), f32[32,3,2,16,256]{4,3,2,1,0:T(8,128)}, u32[]{:S(2)}, u32[]{:S(2)}) async-start(f32[32,3,2,16,256]{4,3,2,1,0:T(8,128)} %bitcast.121), calls=%async_computation | async-start | bytes 6291456 | tf_op jit(solution)/shard_map/all_to_all | solution.py:57
  12.6 3.6 copy.102
  16.9 34.7 %all-to-all-done = f32[32,3,2,16,256]{4,3,2,1,0:T(8,128)} async-done(((f32[32,3,2,16,256]{4,3,2,1,0:T(8,128)}), f32[32,3,2,16,256]{4,3,2,1,0:T(8,128)}, u32[]{:S(2)}, u32[]{:S(2)}) %all-to-all-start) | async-done | bytes 3145760 | tf_op jit(solution)/shard_map/all_to_all | solution.py:57
  51.6 8.5 %all-to-all-start.3 = ((f32[3,2,512,256]{2,1,0,3:T(2,128)}), f32[3,2,512,256]{2,1,0,3:T(2,128)}, u32[]{:S(2)}, u32[]{:S(2)}) async-start(f32[3,2,512,256]{2,1,0,3:T(2,128)} %copy.102), calls=%async_computation.3 | async-start | bytes 6291456 | tf_op jit(solution)/shard_map/all_to_all | solution.py:141
  62.3 3.8 copy.93
  66.1 4.9 %reshape_reshape.3 = f32[3,4,16,32,128]{4,3,2,1,0:T(8,128)} reshape(f32[3,4,16,16,256]{4,3,2,1,0:T(8,128)} %copy.93) | data formatting | bytes 6291456 | tf_op jit(solution)/shard_map/reshape;reshape | solution.py:100
  71.0 7.3 %convolution_bitcast_fusion.1 = f32[3,4,16,64,128]{4,3,2,1,0:T(8,128)S(1)} fusion(f32[3,4,16,32,128]{4,3,2,1,0:T(8,128)} %reshape_reshape.3, f32[32,32]{0,1:T(8,128)S(1)} %get-tuple-element.40, f32[32,32]{0,1:T(8,128)S(1)} %get-tuple-element.41), kind=kOutput, calls=%fused_computation.44 | convolution fusion | flops 603981824 | bytes 9445376 | tf_op jit(solution)/shard_map/kn,...nm->...km/dot_general | solution.py:88
  79.5 5.3 %fusion = f32[3,4,16,32,256]{4,3,2,1,0:T(8,128)S(1)} fusion(f32[3,4,16,32,128]{4,3,2,1,0:T(8,128)S(1)} %get-tuple-element.15, f32[3,4,16,32,128]{4,3,2,1,0:T(8,128)S(1)} %get-tuple-element.14, f32[128,128]{1,0:T(8,128)S(1)} %get-tuple-element.45, f32[128,128]{1,0:T(8,128)S(1)} %get-tuple-element.44, f32[128,128]{1,0:T(8,128)S(1)} %fusion.47), kind=kOutput, calls=%fused_computation | convolution fusion | flops 4833607680 | bytes 12779520 | tf_op jit(solution)/shard_map/...kn,nm->...km/dot_general | solution.py:92
  85.7 5.5 %fusion.4 = f32[3,4,16,32,256]{4,3,2,1,0:T(8,128)S(1)} fusion(f32[3,4,16,32,128]{4,3,2,1,0:T(8,128)S(1)} %get-tuple-element.19, f32[3,4,16,32,128]{4,3,2,1,0:T(8,128)S(1)} %get-tuple-element.18, f32[128,128]{1,0:T(8,128)S(1)} %get-tuple-element.45, f32[128,128]{1,0:T(8,128)S(1)} %fusion.47, f32[128,128]{1,0:T(8,128)S(1)} %get-tuple-element.44), kind=kOutput, calls=%fused_computation.4 | convolution fusion | flops 4833607680 | bytes 12779520 | tf_op jit(solution)/shard_map/...kn,nm->...km/dot_general | solution.py:92
  92.3 3.8 multiply_bitcast_fusion.1
  112.4 16.9 %copy.96 = f32[3,4,16,4096]{2,1,0,3:T(4,128)} copy(f32[3,4,16,4096]{3,2,1,0:T(8,128)S(1)} %pad_maximum_fusion) | data formatting | bytes 6291456 | tf_op jit(solution)/shard_map/stack | solution.py:147
  129.2 23.6 %reshape.184 = f32[16,1,49152]{2,1,0:T(1,128)} reshape(f32[4096,3,4,16]{3,2,1,0:T(4,128)} %bitcast.112) | data formatting | bytes 6291456
  152.8 6.8 %all-to-all-start.1 = ((f32[16,1,49152]{2,1,0:T(1,128)}), f32[16,1,49152]{2,1,0:T(1,128)S(1)}, u32[]{:S(2)}, u32[]{:S(2)}) async-start(f32[16,1,49152]{2,1,0:T(1,128)} %reshape.184), calls=%async_computation.1 | async-start | bytes 6291456 | tf_op jit(solution)/shard_map/all_to_all | solution.py:148
  163.1 5.4 %convolution_bitcast_fusion = f32[3,2,32,64,128]{4,3,2,1,0:T(8,128)S(1)} fusion(f32[3,2,32,32,128]{4,3,2,1,0:T(8,128)S(1)} %bitcast.126, f32[32,32]{0,1:T(8,128)S(1)} %get-tuple-element.40, f32[32,32]{0,1:T(8,128)S(1)} %get-tuple-element.41), kind=kOutput, calls=%fused_computation.43 | convolution fusion | flops 603981824 | bytes 9445376 | tf_op jit(solution)/shard_map/kn,...nm->...km/dot_general | solution.py:88
  169.7 5.5 %fusion.12 = f32[3,2,32,32,256]{4,3,2,1,0:T(8,128)S(1)} fusion(f32[3,2,32,32,128]{4,3,2,1,0:T(8,128)S(1)} %get-tuple-element.11, f32[3,2,32,32,128]{4,3,2,1,0:T(8,128)S(1)} %get-tuple-element.10, f32[128,128]{1,0:T(8,128)S(1)} %get-tuple-element.45, f32[128,128]{1,0:T(8,128)S(1)} %get-tuple-element.44, f32[128,128]{1,0:T(8,128)S(1)} %fusion.47), kind=kOutput, calls=%fused_computation.12 | convolution fusion | flops 4833607680 | bytes 12779520 | tf_op jit(solution)/shard_map/...kn,nm->...km/dot_general | solution.py:92
  176.1 5.3 %fusion.16 = f32[3,2,32,32,256]{4,3,2,1,0:T(8,128)S(1)} fusion(f32[3,2,32,32,128]{4,3,2,1,0:T(8,128)S(1)} %get-tuple-element.17, f32[3,2,32,32,128]{4,3,2,1,0:T(8,128)S(1)} %get-tuple-element.16, f32[128,128]{1,0:T(8,128)S(1)} %get-tuple-element.45, f32[128,128]{1,0:T(8,128)S(1)} %fusion.47, f32[128,128]{1,0:T(8,128)S(1)} %get-tuple-element.44), kind=kOutput, calls=%fused_computation.16 | convolution fusion | flops 4833607680 | bytes 12779520 | tf_op jit(solution)/shard_map/...kn,nm->...km/dot_general | solution.py:92
  182.4 5.2 %multiply_bitcast_fusion = f32[3,2,32,32,128]{4,3,2,1,0:T(8,128)} fusion(f32[3,2,32,32,128]{4,3,2,1,0:T(8,128)S(1)} %get-tuple-element.9, f32[3,2,32,32,128]{4,3,2,1,0:T(8,128)S(1)} %get-tuple-element.8, f32[32,32]{0,1:T(8,128)S(1)} %get-tuple-element.40, f32[32,32]{0,1:T(8,128)S(1)} %get-tuple-element.41), kind=kOutput, calls=%fused_computation.33 | convolution fusion | flops 606341120 | bytes 9445376 | tf_op jit(solution)/shard_map/kn,...nm->...km/dot_general | solution.py:88
  187.7 4.8 %reshape.172 = f32[3,2,32,4096]{3,2,1,0:T(8,128)} reshape(f32[3,2,32,32,128]{4,3,2,1,0:T(8,128)} %multiply_bitcast_fusion) | data formatting | bytes 6291456 | tf_op jit(solution)/shard_map/reshape | solution.py:128
  192.5 4.6 %copy.134 = f32[24,8,8,512]{3,2,1,0:T(8,128)S(1)} copy(f32[24,8,8,512]{3,1,2,0:T(8,128)} %bitcast.125) | data formatting | bytes 6291456
  204.9 10.1 %reduce.5 = f32[16,49152]{1,0:T(8,128)S(1)} reduce(f32[16,1,49152]{2,1,0:T(1,128)} %copy-done.2, f32[]{:T(128)} %broadcast.212), dimensions={1}, to_apply=%all_to_all.47.reduce_sub_computation | reduce | bytes 6291460 | tf_op jit(solution)/shard_map/all_to_all | solution.py:148
  215.0 27.0 %reshape.185 = f32[4096,3,4,16]{3,2,1,0:T(4,128)} reshape(f32[16,49152]{1,0:T(8,128)S(1)} %reduce.5) | data formatting | bytes 6291456
  242.0 19.5 %copy.128 = f32[3,4,16,16,256]{4,2,3,0,1:T(8,128)S(1)} copy(f32[3,4,16,16,256]{2,1,0,4,3:T(4,128)} %bitcast.113) | data formatting | bytes 6291456 | tf_op jit(solution)/shard_map/all_to_all | solution.py:148
  261.5 7.2 %all_to_all.66 = f32[3,4,256,256]{3,2,0,1:T(8,128)} all-to-all(f32[3,4,256,256]{3,2,0,1:T(8,128)S(1)} %bitcast.119), channel_id=1, replica_groups=mesh['plane'=2,'row'=8,'col_0'=4,'col_1'=4] {'plane'}, dimensions={1} | all-to-all | bytes 6291456 | tf_op jit(solution)/shard_map/all_to_all | solution.py:149
  268.8 6.2 %all-to-all-start.4 = ((f32[8,3,2,256,32]{3,4,2,1,0:T(8,128)}), f32[8,3,2,256,32]{3,4,2,1,0:T(8,128)S(1)}, u32[]{:S(2)}, u32[]{:S(2)}) async-start(f32[8,3,2,256,32]{3,4,2,1,0:T(8,128)} %copy.106), calls=%async_computation.4 | async-start | bytes 3145728 | tf_op jit(solution)/shard_map/all_to_all | solution.py:47
  276.6 38.6 %all-to-all-done.4 = f32[8,3,2,256,32]{3,4,2,1,0:T(8,128)S(1)} async-done(((f32[8,3,2,256,32]{3,4,2,1,0:T(8,128)}), f32[8,3,2,256,32]{3,4,2,1,0:T(8,128)S(1)}, u32[]{:S(2)}, u32[]{:S(2)}) %all-to-all-start.4) | async-done | bytes 1572896 | tf_op jit(solution)/shard_map/all_to_all | solution.py:47
  315.2 4.5 %all-to-all-start.5 = ((f32[8,3,2,256,32]{3,4,2,1,0:T(8,128)}), f32[8,3,2,256,32]{3,4,2,1,0:T(8,128)}, u32[]{:S(2)}, u32[]{:S(2)}) async-start(f32[8,3,2,256,32]{3,4,2,1,0:T(8,128)} %copy.107), calls=%async_computation.5 | async-start | bytes 3145728 | tf_op jit(solution)/shard_map/all_to_all | solution.py:47
  322.0 38.1 %all-to-all-done.5 = f32[8,3,2,256,32]{3,4,2,1,0:T(8,128)} async-done(((f32[8,3,2,256,32]{3,4,2,1,0:T(8,128)}), f32[8,3,2,256,32]{3,4,2,1,0:T(8,128)}, u32[]{:S(2)}, u32[]{:S(2)}) %all-to-all-start.5) | async-done | bytes 1572896 | tf_op jit(solution)/shard_map/all_to_all | solution.py:47
  394.9 14.7 %psum.21 = f32[4,4]{1,0:T(4,128)S(1)} all-reduce(f32[4,4]{1,0:T(4,128)S(1)} %multiply_multiply_fusion.1), channel_id=1, replica_groups=mesh['plane'=2,'row'=8,'col_0'=4,'col_1'=4] {'row'}, use_global_device_ids=true, to_apply=%region_4.5 | all-reduce | flops 16 | bytes 128 | tf_op jit(solution)/shard_map/psum | solution.py:67
  409.6 9.3 %psum.22 = f32[4,4]{1,0:T(4,128)S(1)} all-reduce(f32[4,4]{1,0:T(4,128)S(1)} %psum.21), channel_id=1, replica_groups=mesh['plane'=2,'row'=8,'col_0'=4,'col_1'=4] {'col_0'}, use_global_device_ids=true, to_apply=%region_5.6 | all-reduce | flops 16 | bytes 128 | tf_op jit(solution)/shard_map/psum | solution.py:67
  418.9 12.8 %psum.23 = f32[4,4]{1,0:T(4,128)S(1)} all-reduce(f32[4,4]{1,0:T(4,128)S(1)} %psum.22), channel_id=1, replica_groups=mesh['plane'=2,'row'=8,'col_0'=4,'col_1'=4] {'col_1'}, use_global_device_ids=true, to_apply=%region_6.7 | all-reduce | flops 16 | bytes 128 | tf_op jit(solution)/shard_map/psum | solution.py:67
  432.9 3.9 multiply_add_fusion.4
  (81 shorter events, 76.4 us)
Async XLA Ops:
  4.6 7.9 %copy-start.1 = (f32[3,2,512,256]{3,2,1,0:T(8,128)S(1)}, f32[3,2,512,256]{3,2,1,0:T(8,128)}, u32[]{:S(2)}) copy-start(f32[3,2,512,256]{3,2,1,0:T(8,128)} %param.1) | copy-start | bytes 9437188
  4.6 46.9 %all-to-all-start = ((f32[32,3,2,16,256]{4,3,2,1,0:T(8,128)}), f32[32,3,2,16,256]{4,3,2,1,0:T(8,128)}, u32[]{:S(2)}, u32[]{:S(2)}) async-start(f32[32,3,2,16,256]{4,3,2,1,0:T(8,128)} %bitcast.121), calls=%async_computation | async-start | bytes 6291456 | tf_op jit(solution)/shard_map/all_to_all | solution.py:57
  51.6 101.3 %all-to-all-start.3 = ((f32[3,2,512,256]{2,1,0,3:T(2,128)}), f32[3,2,512,256]{2,1,0,3:T(2,128)}, u32[]{:S(2)}, u32[]{:S(2)}) async-start(f32[3,2,512,256]{2,1,0,3:T(2,128)} %copy.102), calls=%async_computation.3 | async-start | bytes 6291456 | tf_op jit(solution)/shard_map/all_to_all | solution.py:141
  104.7 4.1 copy-start
  109.3 1.2 copy-start.9
  109.3 1.5 copy-start.10
  110.9 1.2 copy-start.11
  152.8 49.9 %all-to-all-start.1 = ((f32[16,1,49152]{2,1,0:T(1,128)}), f32[16,1,49152]{2,1,0:T(1,128)S(1)}, u32[]{:S(2)}, u32[]{:S(2)}) async-start(f32[16,1,49152]{2,1,0:T(1,128)} %reshape.184), calls=%async_computation.1 | async-start | bytes 6291456 | tf_op jit(solution)/shard_map/all_to_all | solution.py:148
  202.8 1.7 copy-start.2
  268.8 6.2 %copy-start.7 = (f32[8,3,2,256,32]{3,0,4,2,1:T(8,128)S(1)}, f32[8,3,2,256,32]{3,0,4,2,1:T(8,128)}, u32[]{:S(2)}) copy-start(f32[8,3,2,256,32]{3,0,4,2,1:T(8,128)} %get-tuple-element.28) | copy-start | bytes 4718596
  268.8 46.5 %all-to-all-start.4 = ((f32[8,3,2,256,32]{3,4,2,1,0:T(8,128)}), f32[8,3,2,256,32]{3,4,2,1,0:T(8,128)S(1)}, u32[]{:S(2)}, u32[]{:S(2)}) async-start(f32[8,3,2,256,32]{3,4,2,1,0:T(8,128)} %copy.106), calls=%async_computation.4 | async-start | bytes 3145728 | tf_op jit(solution)/shard_map/all_to_all | solution.py:47
  315.2 4.5 %copy-start.6 = (f32[8,3,2,256,32]{3,4,2,1,0:T(8,128)}, f32[8,3,2,256,32]{3,4,2,1,0:T(8,128)S(1)}, u32[]{:S(2)}) copy-start(f32[8,3,2,256,32]{3,4,2,1,0:T(8,128)S(1)} %all-to-all-done.4) | copy-start | bytes 4718596
  315.2 44.9 %all-to-all-start.5 = ((f32[8,3,2,256,32]{3,4,2,1,0:T(8,128)}), f32[8,3,2,256,32]{3,4,2,1,0:T(8,128)}, u32[]{:S(2)}, u32[]{:S(2)}) async-start(f32[8,3,2,256,32]{3,4,2,1,0:T(8,128)} %copy.107), calls=%async_computation.5 | async-start | bytes 3145728 | tf_op jit(solution)/shard_map/all_to_all | solution.py:47
  382.7 3.2 copy-start.5
  383.8 3.5 copy-start.4
  384.9 3.7 copy-start.3
  388.6 44.3 %copy-start.8 = (f32[1,2,2,256,256]{4,3,2,1,0:T(8,128)S(1)}, f32[1,2,2,256,256]{4,3,2,1,0:T(8,128)}, u32[]{:S(2)}) copy-start(f32[1,2,2,256,256]{4,3,2,1,0:T(8,128)} %copy.101) | copy-start | bytes 3145732
where the time goes:
time: 443 us; the launch traced here: 437 us
  local copies, waits for them, and re-layouts  165 us (37%)
  waiting for transfers between devices  114 us (26%)
  blocking collectives  45.8 us (10%)
  matrix products  43.5 us (10%)
  starting transfers between devices  33.8 us (8%)
  other arithmetic  33.5 us (8%)
    all_to_all x2, waiting for transfers between devices, exchange_in_pieces(): lax.all_to_all(share, axis, split_axis=0, concat_axis=0, tiled=True)  76.7 us
    unnamed x29, local copies, waits for them, and re-layouts  62.9 us
    psum x3, blocking collectives, over_axes(): return functools.reduce(lax.psum, axes, shard)  36.8 us
    all_to_all x1, waiting for transfers between devices, exchange_both(): lax.all_to_all(blocks, axis, split_axis=0, concat_axis=0, tiled=True)  34.7 us
    dot_general x4, matrix products, left_mult(): return jnp.einsum('kn,...nm->...km', coeffs, values, precision=precise)  21.7 us
    dot_general x4, matrix products, right_mult(): return jnp.einsum('...kn,nm->...km', values, coeffs, precision=precise)  21.7 us
    all_to_all x2, local copies, waits for them, and re-layouts, per_device(): lax.all_to_all(packed, COL, split_axis=3, concat_axis=2, tiled=True)  20 us
    another operation x1, local copies, waits for them, and re-layouts, per_device(): packed = jnp.stack([partial_value, slab_y[0], slab_z[0]])  16.9 us
  transfers between devices with their start and end apart: 5, of which 4 were waited for; matrix products, arithmetic and copies ran while one was open for 32% of the time, Pallas kernels for 0%

commit v1 on v0

v1 whole, which is shorter than its diff:
```python
import functools
import math

import jax
import jax.numpy as jnp
import numpy as np
from jax import lax
from jax.experimental import pallas as pl
from jax.experimental.pallas import tpu as pltpu
from jax.sharding import Mesh
from jax.sharding import PartitionSpec as P

N = 4096
FINE = 32
COARSE = 1024
M = 256
ROWS = 8
DISTANCES = (4, 3, 5, 2, 6, 1, 7)
COL = ("col_0", "col_1")
PLANE_COL = ("plane", "col_0", "col_1")
HIGH = lax.Precision.HIGHEST


def toeplitz_parts():
    lags = np.arange(M)[:, None] - np.arange(M)[None, :]
    off = lags != 0
    base = np.zeros((M, M))
    base[off] = (1.0 / 16) * (math.pi / M) * (-1.0) ** lags[off] / np.sin(math.pi * lags[off] / M)
    turn = 2.0 * math.pi / N * (np.arange(16) - 8)[:, None] * np.arange(M)[None, :]
    cos_r, sin_r = np.cos(turn), np.sin(turn)
    cos_c = np.zeros((M, 128))
    sin_c = np.zeros((M, 128))
    cos_c[:, :16] = cos_r.T
    sin_c[:, :16] = sin_r.T
    return [np.asarray(a, np.float32) for a in (base, cos_r, sin_r, cos_c, sin_c)]


def table_kernel(base, cos_r, sin_r, cos_c, sin_c, out):
    left = lax.broadcasted_iota(jnp.int32, (M, M), 0)
    right = lax.broadcasted_iota(jnp.int32, (M, M), 1)
    for k in range(9):
        ca, sa = cos_c[:, k : k + 1], sin_c[:, k : k + 1]
        cb, sb = cos_r[k : k + 1, :], sin_r[k : k + 1, :]
        out[k] = base[...] * (ca * cb + sa * sb)
        if 0 < k < 8:
            middle = 2.0 * math.pi / N * (k - 8) / 16
            out[8 + k] = base[...] * (sa * cb - ca * sb) + jnp.where(left == right, middle, 0.0)


def vmem_call(kernel, outs, scratch=(), smem=0):
    def call(*args):
        specs = [pl.BlockSpec(memory_space=pltpu.SMEM)] * smem
        specs += [pl.BlockSpec(memory_space=pltpu.VMEM)] * (len(args) - smem)
        many = isinstance(outs, (list, tuple))
        out_specs = jax.tree.map(lambda _: pl.BlockSpec(memory_space=pltpu.VMEM), list(outs) if many else outs)
        return pl.pallas_call(
            kernel,
            out_shape=list(outs) if many else outs,
            in_specs=specs,
            out_specs=out_specs,
            scratch_shapes=list(scratch),
        )(*args)

    return call


def f32(*shape):
    return jax.ShapeDtypeStruct(shape, jnp.float32)


def real_dft(values):
    n = len(values)
    if n == 2:
        return [(values[0] + values[1], None), (values[0] - values[1], None)]
    even, odd = real_dft(values[0::2]), real_dft(values[1::2])
    half = n // 2
    out = [None] * (half + 1)
    out[0] = (even[0][0] + odd[0][0], None)
    out[half] = (even[0][0] - odd[0][0], None)
    for k in range(1, n // 4):
        angle = 2.0 * math.pi * k / n
        c, s = math.cos(angle), math.sin(angle)
        (er, ei), (orr, oi) = even[k], odd[k]
        if 2 * k * 4 == n:
            tr, ti = (orr + oi) * c, (oi - orr) * c
        else:
            tr, ti = orr * c + oi * s, oi * c - orr * s
        out[k] = (er + tr, ei + ti)
        out[half - k] = (er - tr, ti - ei)
    q = n // 4
    out[q] = (even[q][0], -odd[q][0])
    return out


def real_idft(spec):
    half = len(spec) - 1
    n = 2 * half
    if n == 2:
        return [spec[0][0] + spec[1][0], spec[0][0] - spec[1][0]]
    q = n // 4
    even, odd = [None] * (q + 1), [None] * (q + 1)
    even[0] = (spec[0][0] + spec[half][0], None)
    odd[0] = (spec[0][0] - spec[half][0], None)
    even[q] = (2.0 * spec[q][0], None)
    odd[q] = (-2.0 * spec[q][1], None)
    for k in range(1, q):
        angle = 2.0 * math.pi * k / n
        c, s = math.cos(angle), math.sin(angle)
        (ar, ai), (br, bi) = spec[k], spec[half - k]
        even[k] = (ar + br, ai - bi)
        dr, di = ar - br, ai + bi
        if 8 * k == n:
            odd[k] = ((dr - di) * c, (dr + di) * c)
        else:
            odd[k] = (dr * c - di * s, dr * s + di * c)
    out = [None] * n
    out[0::2] = real_idft(even)
    out[1::2] = real_idft(odd)
    return out


def lane_ids(rows):
    return lax.broadcasted_iota(jnp.int32, (rows, 128), 1)


def swap_lanes(four):
    group = lax.broadcasted_iota(jnp.int32, four[0].shape, 1) // 32
    low, even = group < 2, lax.rem(group, 2) == 0
    a, b, c, d = four
    a, c = jnp.where(low, a, pltpu.roll(c, 64, 1)), jnp.where(low, pltpu.roll(a, 64, 1), c)
    b, d = jnp.where(low, b, pltpu.roll(d, 64, 1)), jnp.where(low, pltpu.roll(b, 64, 1), d)
    a, b = jnp.where(even, a, pltpu.roll(b, 32, 1)), jnp.where(even, pltpu.roll(a, 96, 1), b)
    c, d = jnp.where(even, c, pltpu.roll(d, 32, 1)), jnp.where(even, pltpu.roll(c, 96, 1), d)
    return a, b, c, d


def pack_rows_kernel(row, *refs, count, step=32):
    vels, outs, held = refs[:count], refs[count : count + 8], refs[count + 8]

    def body(i, carry):
        rows = pl.ds(pl.multiple_of(i * step, step), step)
        later = pl.ds(pl.multiple_of(i * step + 256, step), step)
        for n, vel in enumerate(vels):
            for t in range(2):
                lanes = pl.ds(t * 128, 128)
                four = swap_lanes([vel[0, p, r, lanes] for r in (rows, later) for p in range(2)])
                for off in range(4):
                    held[4 * t + off, n, rows, :] = four[off]
        return carry

    lax.fori_loop(0, 256 // step, body, 0)
    for dist in range(ROWS):
        outs[dist][...] = held[lax.rem(row[0] + dist, ROWS)]


def pack_rows(row, velocity, comps):
    count = len(comps)
    whole = pl.BlockSpec((count, 256, 128), lambda i: (0, 0, 0))

    def one(c):
        return pl.BlockSpec((1, 2, 512, 256), lambda i: (c, 0, 0, 0))

    return pl.pallas_call(
        functools.partial(pack_rows_kernel, count=count),
        out_shape=[f32(count, 256, 128)] * ROWS,
        grid=(1,),
        in_specs=[pl.BlockSpec(memory_space=pltpu.SMEM)] + [one(c) for c in comps],
        out_specs=[whole] * ROWS,
        scratch_shapes=[pltpu.VMEM((ROWS, count, 256, 128), jnp.float32)],
        name="pack_rows",
    )(row, *([velocity] * count))


def hold_blocks(row, blocks, held):
    for dist in range(ROWS):
        held[lax.rem(row[0] + dist, ROWS)] = blocks[dist][0]


def home_tiles(held, rows, t):
    four = swap_lanes([held[4 * t + off, rows, :] for off in range(4)])
    return {(half, p): four[2 * half + p] for half in range(2) for p in range(2)}


def send_blocks(blocks):
    got = [blocks[0]] + [None] * (ROWS - 1)
    for dist in DISTANCES:
        perm = [(i, (i + dist) % ROWS) for i in range(ROWS)]
        got[(ROWS - dist) % ROWS] = lax.ppermute(blocks[dist], "row", perm)
    return got


def spectral_x(table, spec, res):
    res[0, :, :128] = jnp.dot(table[0], spec[0, :, :128], precision=HIGH)
    res[0, :, 128:] = jnp.dot(table[8], spec[0, :, 128:], precision=HIGH)

    def body(k, carry):
        a = jnp.dot(table[k], spec[k], precision=HIGH)
        b = jnp.dot(table[8 + k], spec[k], precision=HIGH)
        res[k, :, :128] = a[:, :128] - b[:, 128:]
        res[k, :, 128:] = a[:, 128:] + b[:, :128]
        return carry

    lax.fori_loop(1, 8, body, 0)


STEP = 16


def store_spec(spec, freq, rows):
    for k in range(8):
        re, im = freq[k]
        spec[k, rows, :128] = re
        spec[k, rows, 128:] = freq[8][0] if k == 0 else im


def load_spec(res, rows):
    freq = [(res[k, rows, :128], res[k, rows, 128:]) for k in range(8)]
    return [(freq[0][0], None)] + freq[1:] + [(freq[0][1], None)]


def grad_v_kernel(table, *refs):
    blocks, outs, spec, res = refs[:8], refs[8:16], refs[16], refs[17]
    low = lane_ids(STEP) < 64

    def forward(i, carry):
        rows = pl.ds(pl.multiple_of(i * STEP, STEP), STEP)
        values = []
        for j in range(8):
            src = blocks[j][0, rows, :]
            values += [src, pltpu.roll(src, 64, 1)]
        store_spec(spec, real_dft(values), rows)
        return carry

    lax.fori_loop(0, 256 // STEP, forward, 0)
    spectral_x(table, spec, res)

    def backward(i, carry):
        rows = pl.ds(pl.multiple_of(i * STEP, STEP), STEP)
        values = real_idft(load_spec(res, rows))
        for j in range(8):
            outs[j][0, rows, :] = jnp.where(low, values[2 * j], pltpu.roll(values[2 * j + 1], 64, 1))
        return carry

    lax.fori_loop(0, 256 // STEP, backward, 0)


X_SCRATCH = (pltpu.VMEM((8, 256, 256), jnp.float32), pltpu.VMEM((8, 256, 256), jnp.float32))


def grad_v(table, blocks):
    return vmem_call(grad_v_kernel, [f32(1, 256, 128)] * 8, X_SCRATCH)(table, *blocks)


def grad_uw_kernel(row, table, *refs):
    blocks, other, out, sums, spec, res = refs[:8], refs[8:16], refs[16], refs[17], refs[18], refs[19]
    lane = lane_ids(STEP)
    low = lane < 64
    first = lax.rem(lane // 32, 2) == 0

    def forward(i, carry):
        rows = pl.ds(pl.multiple_of(i * STEP, STEP), STEP)
        values = []
        for j in range(8):
            u, w = blocks[j][0, rows, :], blocks[j][1, rows, :]
            values += [jnp.where(low, u, pltpu.roll(w, 64, 1)), jnp.where(low, pltpu.roll(u, 64, 1), w)]
        store_spec(spec, real_dft(values), rows)
        return carry

    lax.fori_loop(0, 256 // STEP, forward, 0)
    spectral_x(table, spec, res)

    def backward(i, carry):
        rows = pl.ds(pl.multiple_of(i * STEP, STEP), STEP)
        values = real_idft(load_spec(res, rows))
        totals = []
        for j in range(8):
            a, b = values[2 * j], values[2 * j + 1]
            u_x = jnp.where(low, a, pltpu.roll(b, 64, 1))
            w_x = jnp.where(low, pltpu.roll(a, 64, 1), b)
            diff = blocks[j][0, rows, :] - other[j][0, rows, :]
            u_z = 0.5 * jnp.where(first, pltpu.roll(diff, 96, 1), -pltpu.roll(diff, 32, 1))
            cross = u_z + w_x
            part = u_x * u_x + 0.5 * (cross * cross)
            out[lax.rem(row[0] + j, ROWS), rows, :] = part
            totals.append(carry[j] + part)
        return tuple(totals)

    zero = jnp.zeros((STEP, 128), jnp.float32)
    totals = lax.fori_loop(0, 256 // STEP, backward, (zero,) * 8)
    for j in range(8):
        sums[j : j + 1, :] = jnp.sum(totals[j], axis=0, keepdims=True)


def grad_uw(row, table, other, blocks):
    outs = [f32(8, 256, 128), f32(8, 128)]
    return vmem_call(grad_uw_kernel, outs, X_SCRATCH, smem=1)(row, table, *blocks, *other)


def grad_y_kernel(table, data, out, spec, res):
    def forward(i, carry):
        c = i // 16
        k = lax.rem(i // 8, 2)
        p = lax.rem(i // 4, 2)
        half = pl.ds(pl.multiple_of(lax.rem(i // 2, 2) * 8, 8), 8)
        lanes = pl.ds(pl.multiple_of(lax.rem(i, 2) * 128, 128), 128)
        rows = pl.multiple_of((i // 2) * 8, 8)
        freq = real_dft([data[k, b, c, p, half, lanes] for b in range(16)])
        for f in range(8):
            spec[f, pl.ds(rows, 8), lanes] = freq[f][0]
            spec[f, pl.ds(rows + 192, 8), lanes] = freq[8][0] if f == 0 else freq[f][1]
        return carry

    lax.fori_loop(0, 48, forward, 0)
    res[0, :192] = jnp.dot(spec[0, :192], table[0], precision=HIGH) * -1.0
    res[0, 192:] = jnp.dot(spec[0, 192:], table[8], precision=HIGH) * -1.0

    def middle(f, carry):
        a = jnp.dot(spec[f], table[f], precision=HIGH)
        b = jnp.dot(spec[f], table[8 + f], precision=HIGH)
        res[f, :192] = -a[:192] - b[192:]
        res[f, 192:] = b[:192] - a[192:]
        return carry

    lax.fori_loop(1, 8, middle, 0)

    def backward(i, carry):
        k = i // 4
        half = pl.ds(pl.multiple_of(lax.rem(i // 2, 2) * 8, 8), 8)
        lanes = pl.ds(pl.multiple_of(lax.rem(i, 2) * 128, 128), 128)
        for p in range(2):

            def slope(c):
                start = pl.multiple_of(c * 64 + k * 32 + p * 16 + lax.rem(i // 2, 2) * 8, 8)
                freq = [(res[f, pl.ds(start, 8), lanes], res[f, pl.ds(start + 192, 8), lanes]) for f in range(8)]
                return real_idft([(freq[0][0], None)] + freq[1:] + [(freq[0][1], None)])

            def slope_z(c, b):
                gap = data[k, b, c, 1 - p, half, lanes] - data[1 - k, b, c, 1 - p, half, lanes]
                return gap * (0.5 if p == 0 else -0.5)

            for b, value in enumerate(slope(0)):
                out[k, b, 1, p, half, lanes] = value
            for b, value in enumerate(slope(1)):
                w_z = slope_z(2, b)
                out[k, b, 0, p, half, lanes] = value * value + w_z * w_z
            for b, value in enumerate(slope(2)):
                cross = slope_z(1, b) + value
                out[k, b, 0, p, half, lanes] += 0.5 * (cross * cross)
        return carry

    lax.fori_loop(0, 8, backward, 0)


def grad_y(table, data):
    scratch = (pltpu.VMEM((8, 384, 256), jnp.float32), pltpu.VMEM((8, 384, 256), jnp.float32))
    return vmem_call(grad_y_kernel, f32(2, 16, 2, 2, 16, 256), scratch)(table, data)


def pack_cols_kernel(vel, out):
    def body(g, carry):
        start = pl.multiple_of(g * 16, 16)
        for c in range(3):
            for p in range(2):
                out[g, c, p] = vel[c, p, pl.ds(start, 16), :]
        return carry

    lax.fori_loop(0, 32, body, 0)


def partial_kernel(place, y_terms, x_sums, *refs):
    blocks, out, boxes, held = refs[:8], refs[8], refs[9], refs[10]
    hold_blocks(place, blocks, held)

    def body(i, carry):
        rows = pl.ds(pl.multiple_of(i * 16, 16), 16)
        for t in range(2):
            lanes = pl.ds(t * 128, 128)
            for (half, p), v_x in home_tiles(held, rows, t).items():
                g = i + 16 * half
                cross = y_terms[g, 1, p, :, lanes] + v_x
                value = y_terms[g, 0, p, :, lanes] + 0.5 * (cross * cross)
                out[p, pl.ds(pl.multiple_of(g * 16, 16), 16), lanes] = value
                carry = carry + value
        return carry

    total = lax.fori_loop(0, 16, body, jnp.zeros((16, 128), jnp.float32))
    down = lax.broadcasted_iota(jnp.int32, (8, 128), 0)
    mine = lax.broadcasted_iota(jnp.int32, (8, 128), 1) == place[1] // 4
    zero = jnp.zeros((8, 128), jnp.float32)
    found = jnp.where(down == place[0] // 2, jnp.sum(total), zero)
    for j in range(ROWS):
        box = lax.rem(place[0] + j, ROWS) // 2
        found = found + jnp.where(down == box, jnp.sum(x_sums[j : j + 1, :]), zero)
    boxes[...] = jnp.where(mine, found * (1.0 / (4 * COARSE * COARSE)), zero)


def final_kernel(part, select, held, out, boxes, lines):

    def body(a, carry):
        rows = pl.ds(pl.multiple_of(a * 32, 32), 32)
        for t in range(2):
            lanes = pl.ds(t * 128, 128)
            tiles = home_tiles(held, rows, t)
            for half in range(2):
                there = pl.ds(pl.multiple_of(a * 32 + 256 * half, 32), 32)
                first = part[0, there, lanes] + tiles[half, 0]
                second = part[1, there, lanes] + tiles[half, 1]
                out[0, there, lanes] = first
                out[1, there, lanes] = second
                total = (first + second).reshape(4, 8, 128).sum(axis=0)
                lines[a + 8 * half, :, lanes] = total
        return carry

    lax.fori_loop(0, 8, body, 0)
    boxes[...] = jnp.dot(jnp.sum(lines[...], axis=1), select[...], precision=HIGH)


def whole_step(velocity):
    row = lax.axis_index("row")
    col = lax.axis_index(COL)
    row_arg = row.astype(jnp.int32).reshape(1)
    parts = [jnp.asarray(a) for a in toeplitz_parts()]
    for_cols = vmem_call(pack_cols_kernel, f32(32, 3, 2, 16, 256))(velocity)
    lines = lax.all_to_all(for_cols, PLANE_COL, split_axis=0, concat_axis=0, tiled=True)
    v_blocks = pack_rows(row_arg, velocity, (1,))
    v_blocks = send_blocks(v_blocks)
    uw_blocks = pack_rows(row_arg, velocity, (0, 2))
    uw_blocks = send_blocks(uw_blocks)
    table = vmem_call(table_kernel, f32(16, M, M))(*parts)
    v_x = grad_v(table, v_blocks)
    v_x = send_blocks(v_x)
    y_terms = grad_y(table, lines.reshape(2, 16, 3, 2, 16, 256))
    y_terms = lax.all_to_all(
        y_terms.reshape(32, 2, 2, 16, 256), PLANE_COL, split_axis=0, concat_axis=0, tiled=True
    )
    other = [lax.ppermute(b, "plane", [(0, 1), (1, 0)]) for b in uw_blocks]
    x_terms, x_sums = grad_uw(row_arg, table, other, uw_blocks)
    x_terms = lax.all_to_all(x_terms, "row", split_axis=0, concat_axis=0, tiled=True)
    held = pltpu.VMEM((ROWS, 256, 128), jnp.float32)
    place = jnp.stack([row, col]).astype(jnp.int32)
    part, coarse = vmem_call(partial_kernel, [f32(2, 512, 256), f32(8, 128)], (held,), smem=1)(
        place, y_terms, x_sums, *v_x
    )
    coarse = sum_of_four(coarse, ("plane", "row"), lambda i, n: i ^ (8, 1, 9)[n])
    coarse = sum_of_four(coarse, "row", lambda i, n: (i + (4, 2, 6)[n]) % 8)
    coarse = sum_of_four(coarse, "col_1", lambda i, n: (i + (2, 1, 3)[n]) % 4)
    coarse = sum_of_four(coarse, "col_0", lambda i, n: (i + (2, 1, 3)[n]) % 4)
    coarse = coarse[:4, :4]
    select = np.zeros((256, 128), np.float32)
    select[np.arange(256), np.arange(256) // FINE] = 1.0 / (4 * FINE * FINE)
    coarse, part = lax.optimization_barrier((coarse, part))
    dissip, fine = vmem_call(
        final_kernel,
        [f32(2, 512, 256), f32(16, 128)],
        (pltpu.VMEM((16, 8, 256), jnp.float32),),
    )(part, jnp.asarray(select), x_terms)
    fine = (fine + lax.ppermute(fine, "plane", [(0, 1), (1, 0)]))[:, :8]
    return dissip, fine, coarse


def sum_of_four(values, axis, partner):
    size = lax.axis_size(axis)
    got = [lax.ppermute(values, axis, [(i, partner(i, n)) for i in range(size)]) for n in range(3)]
    return (values + got[0]) + (got[1] + got[2])


def solution(mesh):
    split = Mesh(
        mesh.devices.reshape(mesh.shape["plane"], mesh.shape["row"], 4, 4),
        ("plane", "row", "col_0", "col_1"),
    )
    in_specs = (P(None, "plane", "row", COL),)
    out_specs = (P("plane", "row", COL), P("row", COL), P())
    return jax.shard_map(whole_step, mesh=split, in_specs=in_specs, out_specs=out_specs, check_vma=False)
```

time: 443 us -> 301 us (0.68)
  local copies, waits for them, and re-layouts: 165 us -> 5.56 us
  Pallas kernels: 0 us -> 65.8 us
  blocking collectives: 45.8 us -> 0 us
  matrix products: 43.5 us -> 0 us
  starting transfers between devices: 33.8 us -> 76.4 us
  waiting for transfers between devices: 114 us -> 148 us
  other arithmetic: 33.5 us -> 1.97 us
    ppermute x0 -> x42, waiting for transfers between devices: none -> 113 us  [the longest x21 97.3 us: send_blocks(): got[(ROWS - dist) % ROWS] = lax.ppermute(blocks[dist], 'row', perm)]
    all_to_all x5 -> x3, waiting for transfers between devices: 114 us -> 35 us  [the longest x1 35 us: whole_step(): lax.all_to_all(for_cols, PLANE_COL, split_axis=0, concat_axis=0, tiled=True)]
    pallas_call x0 -> x9, Pallas kernels: none -> 65.8 us  [the longest x7 56.6 us: call(): pl.pallas_call(kernel, out_shape=list(outs) if many else outs, in_specs=s...]
    ppermute x0 -> x42, starting transfers between devices: none -> 58.7 us  [the longest x21 38.3 us: send_blocks(): got[(ROWS - dist) % ROWS] = lax.ppermute(blocks[dist], 'row', perm)]
    unnamed x29 -> x55, local copies, waits for them, and re-layouts: 62.9 us -> 4.98 us
    dot_general x8 -> x0, matrix products: 43.5 us -> none  [the longest x4 21.7 us: left_mult(): return jnp.einsum('kn,...nm->...km', coeffs, values, precision=precise)]
    psum x3 -> x0, blocking collectives: 36.8 us -> none  [over_axes(): return functools.reduce(lax.psum, axes, shard)]
    another operation x3 -> x0, local copies, waits for them, and re-layouts: 25.8 us -> none  [the longest x1 16.9 us: per_device(): packed = jnp.stack([partial_value, slab_y[0], slab_z[0]])]
  transfers between devices with their start and end apart: 5 -> 45, of which waited for: 4 -> 26; matrix products, arithmetic and copies ran while one was open for 32% -> 1% of each run, Pallas kernels for 0% -> 15%
where the time goes in v1:
time: 301 us; the launch traced here: 298 us
  waiting for transfers between devices  148 us (49%)
  starting transfers between devices  76.4 us (25%)
  Pallas kernels  65.8 us (22%)
  local copies, waits for them, and re-layouts  5.56 us (2%)
    ppermute x21, waiting for transfers between devices, send_blocks(): got[(ROWS - dist) % ROWS] = lax.ppermute(blocks[dist], 'row', perm)  97.3 us
    pallas_call x7, Pallas kernels, call(): pl.pallas_call(kernel, out_shape=list(outs) if many else outs, in_specs=s...  56.6 us
    ppermute x21, starting transfers between devices, send_blocks(): got[(ROWS - dist) % ROWS] = lax.ppermute(blocks[dist], 'row', perm)  38.3 us
    all_to_all x1, waiting for transfers between devices, whole_step(): lax.all_to_all(for_cols, PLANE_COL, split_axis=0, concat_axis=0, tiled=True)  35 us
    ppermute x12, starting transfers between devices, sum_of_four(): lax.ppermute(values, axis, [(i, partner(i, n)) for i in range(size)])  18.7 us
    ppermute x12, waiting for transfers between devices, sum_of_four(): lax.ppermute(values, axis, [(i, partner(i, n)) for i in range(size)])  12.7 us
    pallas_call x2, Pallas kernels, pack_rows(): pl.pallas_call(functools.partial(pack_rows_kernel, count=count), out_shap...  9.15 us
    all_to_all x1, starting transfers between devices, whole_step(): lax.all_to_all(for_cols, PLANE_COL, split_axis=0, concat_axis=0, tiled=True)  7.62 us
  transfers between devices with their start and end apart: 45, of which 26 were waited for; matrix products, arithmetic and copies ran while one was open for 1% of the time, Pallas kernels for 15%

profile of v1, /device:TPU:2, one launch (start us, length us, event | category | flops | bytes accessed | tf_op | source)
XLA Modules:
  0.0 298.1 jit_solution(95588629840356554)
XLA Ops:
  0.6 3.9 %shard_map.95 = f32[32,3,2,16,256]{4,3,2,1,0:T(8,128)} custom-call(f32[3,2,512,256]{3,2,1,0:T(8,128)} %refs_0_.3), custom_call_target="tpu_custom_call" | custom-call | tf_op jit(solution)/shard_map/pallas_call | solution.py:56
  4.5 7.6 %all-to-all-start = ((f32[32,3,2,16,256]{4,3,2,1,0:T(8,128)}), f32[32,3,2,16,256]{4,3,2,1,0:T(8,128)S(1)}, u32[]{:S(2)}, u32[]{:S(2)}) async-start(f32[32,3,2,16,256]{4,3,2,1,0:T(8,128)} %shard_map.95), calls=%async_computation | async-start | bytes 6291456 | tf_op jit(solution)/shard_map/all_to_all | solution.py:424
  12.1 3.9 %shard_map.94.table = f32[16,256,256]{2,1,0:T(8,128)} custom-call(f32[256,256]{1,0:T(8,128)} %constant.27.clone.base, f32[16,256]{1,0:T(8,128)} %constant.28.clone.cos_r, f32[16,256]{1,0:T(8,128)} %constant.29.clone.sin_r, f32[256,128]{1,0:T(8,128)} %constant.30.clone.cos_c, f32[256,128]{1,0:T(8,128)} %constant.31.clone.sin_c), custom_call_target="tpu_custom_call" | custom-call | tf_op jit(solution)/shard_map/pallas_call | solution.py:56
  16.0 35.0 %all-to-all-done = f32[32,3,2,16,256]{4,3,2,1,0:T(8,128)S(1)} async-done(((f32[32,3,2,16,256]{4,3,2,1,0:T(8,128)}), f32[32,3,2,16,256]{4,3,2,1,0:T(8,128)S(1)}, u32[]{:S(2)}, u32[]{:S(2)}) %all-to-all-start) | async-done | bytes 3145760 | tf_op jit(solution)/shard_map/all_to_all | solution.py:424
  52.7 14.3 %shard_map.96 = f32[2,16,2,2,16,256]{5,4,3,2,1,0:T(8,128)} custom-call(f32[16,256,256]{2,1,0:T(8,128)} %shard_map.94.table, f32[2,16,3,2,16,256]{5,4,3,2,1,0:T(8,128)} %bitcast.4), custom_call_target="tpu_custom_call" | custom-call | tf_op jit(solution)/shard_map/pallas_call | solution.py:56
  67.0 6.5 %all-to-all-start.1 = ((f32[32,2,2,16,256]{4,3,2,1,0:T(8,128)}), f32[32,2,2,16,256]{4,3,2,1,0:T(8,128)S(1)}, u32[]{:S(2)}, u32[]{:S(2)}) async-start(f32[32,2,2,16,256]{4,3,2,1,0:T(8,128)} %bitcast.5), calls=%async_computation.1 | async-start | bytes 4194304 | tf_op jit(solution)/shard_map/all_to_all | solution.py:433
  73.5 5.3 %pack_rows.2 = (f32[2,256,128]{2,1,0:T(8,128)}, f32[2,256,128]{2,1,0:T(8,128)}, f32[2,256,128]{2,1,0:T(8,128)}, f32[2,256,128]{2,1,0:T(8,128)}, f32[2,256,128]{2...) custom-call(s32[1]{0:T(128)} %bitcast.row, f32[3,2,512,256]{3,2,1,0:T(8,128)} %refs_0_.3, ...), custom_call_target="tpu_custom_call" | custom-call | tf_op jit(solution)/shard_map/pack_rows/pallas_call | solution.py:163
  78.9 5.9 %collective-permute-start = (f32[2,256,128]{2,1,0:T(8,128)}, f32[2,256,128]{2,1,0:T(8,128)S(1)}, u32[]{:S(2)}, u32[]{:S(2)}) collective-permute-start(f32[2,256,128]{2,1,0:T(8,128)} %get-tuple-element.36), channel_id=1, source_target_pairs={{0,112},{16,0},{32,16},{48,32},{64,48},{80,64},{96,80},{112,96},{1... | collective-permute-start | bytes 786440 | tf_op jit(solution)/shard_map/ppermute | solution.py:188
  86.6 5.0 %collective-permute-start.3 = (f32[2,256,128]{2,1,0:T(8,128)}, f32[2,256,128]{2,1,0:T(8,128)S(1)}, u32[]{:S(2)}, u32[]{:S(2)}) collective-permute-start(f32[2,256,128]{2,1,0:T(8,128)} %get-tuple-element.39), channel_id=1, source_target_pairs={{0,64},{16,80},{32,96},{48,112},{64,0},{80,16},{96,32},{112,48},{1... | collective-permute-start | bytes 786440 | tf_op jit(solution)/shard_map/ppermute | solution.py:188
  91.7 6.8 %collective-permute-done.refs_1_ = f32[2,256,128]{2,1,0:T(8,128)S(1)} collective-permute-done((f32[2,256,128]{2,1,0:T(8,128)}, f32[2,256,128]{2,1,0:T(8,128)S(1)}, u32[]{:S(2)}, u32[]{:S(2)}) %collective-permute-start) | collective-permute-done | bytes 262176 | tf_op jit(solution)/shard_map/ppermute | solution.py:188
  98.5 12.8 %collective-permute-done.1.refs_2_ = f32[2,256,128]{2,1,0:T(8,128)S(1)} collective-permute-done((f32[2,256,128]{2,1,0:T(8,128)}, f32[2,256,128]{2,1,0:T(8,128)S(1)}, u32[]{:S(2)}, u32[]{:S(2)}) %collective-permute-start.1) | collective-permute-done | bytes 262176 | tf_op jit(solution)/shard_map/ppermute | solution.py:188
  111.2 19.0 %collective-permute-done.2.refs_3_ = f32[2,256,128]{2,1,0:T(8,128)S(1)} collective-permute-done((f32[2,256,128]{2,1,0:T(8,128)}, f32[2,256,128]{2,1,0:T(8,128)S(1)}, u32[]{:S(2)}, u32[]{:S(2)}) %collective-permute-start.2) | collective-permute-done | bytes 262176 | tf_op jit(solution)/shard_map/ppermute | solution.py:188
  134.1 3.6 %collective-permute-done.6.refs_7_ = f32[2,256,128]{2,1,0:T(8,128)S(1)} collective-permute-done((f32[2,256,128]{2,1,0:T(8,128)}, f32[2,256,128]{2,1,0:T(8,128)S(1)}, u32[]{:S(2)}, u32[]{:S(2)}) %collective-permute-start.6) | collective-permute-done | bytes 262176 | tf_op jit(solution)/shard_map/ppermute | solution.py:188
  141.1 13.4 %shard_map.97 = (f32[8,256,128]{2,1,0:T(8,128)}, f32[8,128]{1,0:T(8,128)}) custom-call(s32[1]{0:T(128)} %bitcast.row, f32[16,256,256]{2,1,0:T(8,128)} %shard_map.94.table, f32[2,256,128]{2,1,0:T(8,128)} %get-tuple-element.35.refs_0_, f32[2,256,128]{2,1,0:T(8,128)} %copy-done.3, f32[2,256,128]{2,1,0:T(8,128)} %copy-done.4, f32[2,256,128]{2,1,0:T(8,128)} %copy-done.5, ...), custom_call_target="tpu_custom_call" | custom-call | tf_op jit(solution)/shard_map/pallas_call | solution.py:56
  154.6 3.6 %all-to-all-start.2 = ((f32[8,256,128]{2,1,0:T(8,128)}), f32[8,256,128]{2,1,0:T(8,128)S(1)}, u32[]{:S(2)}, u32[]{:S(2)}) async-start(f32[8,256,128]{2,1,0:T(8,128)} %get-tuple-element.63), calls=%async_computation.2 | async-start | bytes 2097152 | tf_op jit(solution)/shard_map/all_to_all | solution.py:438
  158.1 3.8 %pack_rows.3 = (f32[1,256,128]{2,1,0:T(8,128)}, f32[1,256,128]{2,1,0:T(8,128)}, f32[1,256,128]{2,1,0:T(8,128)}, f32[1,256,128]{2,1,0:T(8,128)}, f32[1,256,128]{2...) custom-call(s32[1]{0:T(128)} %bitcast.row, f32[3,2,512,256]{3,2,1,0:T(8,128)} %refs_0_.3), custom_call_target="tpu_custom_call" | custom-call | tf_op jit(solution)/shard_map/pack_rows/pallas_call | solution.py:163
  168.9 3.6 %collective-permute-start.18 = (f32[1,256,128]{2,1,0:T(8,128)}, f32[1,256,128]{2,1,0:T(8,128)}, u32[]{:S(2)}, u32[]{:S(2)}) collective-permute-start(f32[1,256,128]{2,1,0:T(8,128)} %get-tuple-element.48), channel_id=1, source_target_pairs={{0,64},{16,80},{32,96},{48,112},{64,0},{80,16},{96,32},{112,48},{1... | collective-permute-start | bytes 393224 | tf_op jit(solution)/shard_map/ppermute | solution.py:188
  172.7 15.0 %collective-permute-done.15.refs_1_ = f32[1,256,128]{2,1,0:T(8,128)S(1)} collective-permute-done((f32[1,256,128]{2,1,0:T(8,128)}, f32[1,256,128]{2,1,0:T(8,128)S(1)}, u32[]{:S(2)}, u32[]{:S(2)}) %collective-permute-start.15) | collective-permute-done | bytes 131104 | tf_op jit(solution)/shard_map/ppermute | solution.py:188
  189.5 6.8 %collective-permute-done.16.refs_2_ = f32[1,256,128]{2,1,0:T(8,128)S(1)} collective-permute-done((f32[1,256,128]{2,1,0:T(8,128)}, f32[1,256,128]{2,1,0:T(8,128)S(1)}, u32[]{:S(2)}, u32[]{:S(2)}) %collective-permute-start.16) | collective-permute-done | bytes 131104 | tf_op jit(solution)/shard_map/ppermute | solution.py:188
  196.3 5.9 %collective-permute-done.17.refs_3_ = f32[1,256,128]{2,1,0:T(8,128)S(1)} collective-permute-done((f32[1,256,128]{2,1,0:T(8,128)}, f32[1,256,128]{2,1,0:T(8,128)S(1)}, u32[]{:S(2)}, u32[]{:S(2)}) %collective-permute-start.17) | collective-permute-done | bytes 131104 | tf_op jit(solution)/shard_map/ppermute | solution.py:188
  202.2 3.6 %collective-permute-done.20.refs_6_ = f32[1,256,128]{2,1,0:T(8,128)} collective-permute-done((f32[1,256,128]{2,1,0:T(8,128)}, f32[1,256,128]{2,1,0:T(8,128)}, u32[]{:S(2)}, u32[]{:S(2)}) %collective-permute-start.20) | collective-permute-done | bytes 131104 | tf_op jit(solution)/shard_map/ppermute | solution.py:188
  207.3 11.5 %shard_map.98 = (f32[1,256,128]{2,1,0:T(8,128)}, f32[1,256,128]{2,1,0:T(8,128)}, f32[1,256,128]{2,1,0:T(8,128)}, f32[1,256,128]{2,1,0:T(8,128)}, f32[1,256,128]{...) custom-call(f32[16,256,256]{2,1,0:T(8,128)} %shard_map.94.table, ...), custom_call_target="tpu_custom_call" | custom-call | tf_op jit(solution)/shard_map/pallas_call | solution.py:56
  223.9 3.8 %collective-permute-start.25 = (f32[1,256,128]{2,1,0:T(8,128)}, f32[1,256,128]{2,1,0:T(8,128)S(1)}, u32[]{:S(2)}, u32[]{:S(2)}) collective-permute-start(f32[1,256,128]{2,1,0:T(8,128)} %get-tuple-element.56), channel_id=1, source_target_pairs={{0,64},{16,80},{32,96},{48,112},{64,0},{80,16},{96,32},{112,48},{1... | collective-permute-start | bytes 393224 | tf_op jit(solution)/shard_map/ppermute | solution.py:188
  227.7 3.3 %collective-permute-start.26 = (f32[1,256,128]{2,1,0:T(8,128)}, f32[1,256,128]{2,1,0:T(8,128)S(1)}, u32[]{:S(2)}, u32[]{:S(2)}) collective-permute-start(f32[1,256,128]{2,1,0:T(8,128)} %get-tuple-element.57), channel_id=1, source_target_pairs={{0,48},{16,64},{32,80},{48,96},{64,112},{80,0},{96,16},{112,32},{1... | collective-permute-start | bytes 393224 | tf_op jit(solution)/shard_map/ppermute | solution.py:188
  231.8 6.9 %collective-permute-done.23.refs_2_ = f32[1,256,128]{2,1,0:T(8,128)S(1)} collective-permute-done((f32[1,256,128]{2,1,0:T(8,128)}, f32[1,256,128]{2,1,0:T(8,128)S(1)}, u32[]{:S(2)}, u32[]{:S(2)}) %collective-permute-start.23) | collective-permute-done | bytes 131104 | tf_op jit(solution)/shard_map/ppermute | solution.py:188
  241.0 5.3 %collective-permute-done.26.refs_5_ = f32[1,256,128]{2,1,0:T(8,128)S(1)} collective-permute-done((f32[1,256,128]{2,1,0:T(8,128)}, f32[1,256,128]{2,1,0:T(8,128)S(1)}, u32[]{:S(2)}, u32[]{:S(2)}) %collective-permute-start.26) | collective-permute-done | bytes 131104 | tf_op jit(solution)/shard_map/ppermute | solution.py:188
  247.5 4.0 %collective-permute-done.28.refs_7_ = f32[1,256,128]{2,1,0:T(8,128)S(1)} collective-permute-done((f32[1,256,128]{2,1,0:T(8,128)}, f32[1,256,128]{2,1,0:T(8,128)S(1)}, u32[]{:S(2)}, u32[]{:S(2)}) %collective-permute-start.28) | collective-permute-done | bytes 131104 | tf_op jit(solution)/shard_map/ppermute | solution.py:188
  252.1 5.6 %shard_map.99 = (f32[2,512,256]{2,1,0:T(8,128)}, f32[8,128]{1,0:T(8,128)}) custom-call(s32[2]{0:T(128)} %pad_add_fusion.place, f32[32,2,2,16,256]{4,3,2,1,0:T(8,128)} %copy-done.1, f32[8,128]{1,0:T(8,128)} %get-tuple-element.43.x_sums, f32[1,256,128]{2,1,0:T(8,128)} %get-tuple-element.52.refs_0_, f32[1,256,128]{2,1,0:T(8,128)} %copy-done.20, ...), custom_call_target="tpu_custom_call" | custom-call | tf_op jit(solution)/shard_map/pallas_call | solution.py:56
  266.8 3.3 %collective-permute-start.32 = (f32[8,128]{1,0:T(8,128)S(1)}, f32[8,128]{1,0:T(8,128)S(1)}, u32[]{:S(2)}, u32[]{:S(2)}) collective-permute-start(f32[8,128]{1,0:T(8,128)S(1)} %add_add_fusion.3), channel_id=1, source_target_pairs={{0,64},{16,80},{32,96},{48,112},{64,0},{80,16},{96,32},{112,48},{1... | collective-permute-start | bytes 12296 | tf_op jit(solution)/shard_map/ppermute | solution.py:463
  270.1 4.2 %collective-permute-done.32 = f32[8,128]{1,0:T(8,128)S(1)} collective-permute-done((f32[8,128]{1,0:T(8,128)S(1)}, f32[8,128]{1,0:T(8,128)S(1)}, u32[]{:S(2)}, u32[]{:S(2)}) %collective-permute-start.32) | collective-permute-done | bytes 4128 | tf_op jit(solution)/shard_map/ppermute | solution.py:463
  286.5 3.3 %collective-permute-done.38 = f32[8,128]{1,0:T(8,128)S(1)} collective-permute-done((f32[8,128]{1,0:T(8,128)S(1)}, f32[8,128]{1,0:T(8,128)S(1)}, u32[]{:S(2)}, u32[]{:S(2)}) %collective-permute-start.38) | collective-permute-done | bytes 4128 | tf_op jit(solution)/shard_map/ppermute | solution.py:463
  291.3 4.0 %shard_map.100 = (f32[2,512,256]{2,1,0:T(8,128)}, f32[16,128]{1,0:T(8,128)}) custom-call(f32[2,512,256]{2,1,0:T(8,128)} %get-tuple-element.62.part, f32[256,128]{1,0:T(8,128)} %constant.32.clone.select, f32[8,256,128]{2,1,0:T(8,128)} %copy-done.2), custom_call_target="tpu_custom_call" | custom-call | tf_op jit(solution)/shard_map/pallas_call | solution.py:56
  (129 shorter events, 56.8 us)
Async XLA Ops:
  4.5 46.6 %all-to-all-start = ((f32[32,3,2,16,256]{4,3,2,1,0:T(8,128)}), f32[32,3,2,16,256]{4,3,2,1,0:T(8,128)S(1)}, u32[]{:S(2)}, u32[]{:S(2)}) async-start(f32[32,3,2,16,256]{4,3,2,1,0:T(8,128)} %shard_map.95), calls=%async_computation | async-start | bytes 6291456 | tf_op jit(solution)/shard_map/all_to_all | solution.py:424
  67.0 87.6 %all-to-all-start.1 = ((f32[32,2,2,16,256]{4,3,2,1,0:T(8,128)}), f32[32,2,2,16,256]{4,3,2,1,0:T(8,128)S(1)}, u32[]{:S(2)}, u32[]{:S(2)}) async-start(f32[32,2,2,16,256]{4,3,2,1,0:T(8,128)} %bitcast.5), calls=%async_computation.1 | async-start | bytes 4194304 | tf_op jit(solution)/shard_map/all_to_all | solution.py:433
  78.9 19.6 %collective-permute-start = (f32[2,256,128]{2,1,0:T(8,128)}, f32[2,256,128]{2,1,0:T(8,128)S(1)}, u32[]{:S(2)}, u32[]{:S(2)}) collective-permute-start(f32[2,256,128]{2,1,0:T(8,128)} %get-tuple-element.36), channel_id=1, source_target_pairs={{0,112},{16,0},{32,16},{48,32},{64,48},{80,64},{96,80},{112,96},{1... | collective-permute-start | bytes 786440 | tf_op jit(solution)/shard_map/ppermute | solution.py:188
  84.7 26.5 %collective-permute-start.1 = (f32[2,256,128]{2,1,0:T(8,128)}, f32[2,256,128]{2,1,0:T(8,128)S(1)}, u32[]{:S(2)}, u32[]{:S(2)}) collective-permute-start(f32[2,256,128]{2,1,0:T(8,128)} %get-tuple-element.37), channel_id=1, source_target_pairs={{0,96},{16,112},{32,0},{48,16},{64,32},{80,48},{96,64},{112,80},{1... | collective-permute-start | bytes 786440 | tf_op jit(solution)/shard_map/ppermute | solution.py:188
  86.2 44.0 %collective-permute-start.2 = (f32[2,256,128]{2,1,0:T(8,128)}, f32[2,256,128]{2,1,0:T(8,128)S(1)}, u32[]{:S(2)}, u32[]{:S(2)}) collective-permute-start(f32[2,256,128]{2,1,0:T(8,128)} %get-tuple-element.38), channel_id=1, source_target_pairs={{0,80},{16,96},{32,112},{48,0},{64,16},{80,32},{96,48},{112,64},{1... | collective-permute-start | bytes 786440 | tf_op jit(solution)/shard_map/ppermute | solution.py:188
  86.6 43.6 %collective-permute-start.3 = (f32[2,256,128]{2,1,0:T(8,128)}, f32[2,256,128]{2,1,0:T(8,128)S(1)}, u32[]{:S(2)}, u32[]{:S(2)}) collective-permute-start(f32[2,256,128]{2,1,0:T(8,128)} %get-tuple-element.39), channel_id=1, source_target_pairs={{0,64},{16,80},{32,96},{48,112},{64,0},{80,16},{96,32},{112,48},{1... | collective-permute-start | bytes 786440 | tf_op jit(solution)/shard_map/ppermute | solution.py:188
  91.7 39.1 %collective-permute-start.4 = (f32[2,256,128]{2,1,0:T(8,128)}, f32[2,256,128]{2,1,0:T(8,128)S(1)}, u32[]{:S(2)}, u32[]{:S(2)}) collective-permute-start(f32[2,256,128]{2,1,0:T(8,128)} %get-tuple-element.40), channel_id=1, source_target_pairs={{0,48},{16,64},{32,80},{48,96},{64,112},{80,0},{96,16},{112,32},{1... | collective-permute-start | bytes 786440 | tf_op jit(solution)/shard_map/ppermute | solution.py:188
  98.5 35.6 %collective-permute-start.5 = (f32[2,256,128]{2,1,0:T(8,128)}, f32[2,256,128]{2,1,0:T(8,128)S(1)}, u32[]{:S(2)}, u32[]{:S(2)}) collective-permute-start(f32[2,256,128]{2,1,0:T(8,128)} %get-tuple-element.41), channel_id=1, source_target_pairs={{0,32},{16,48},{32,64},{48,80},{64,96},{80,112},{96,0},{112,16},{1... | collective-permute-start | bytes 786440 | tf_op jit(solution)/shard_map/ppermute | solution.py:188
  111.2 26.5 %collective-permute-start.6 = (f32[2,256,128]{2,1,0:T(8,128)}, f32[2,256,128]{2,1,0:T(8,128)S(1)}, u32[]{:S(2)}, u32[]{:S(2)}) collective-permute-start(f32[2,256,128]{2,1,0:T(8,128)} %get-tuple-element.42), channel_id=1, source_target_pairs={{0,16},{16,32},{32,48},{48,64},{64,80},{80,96},{96,112},{112,0},{1... | collective-permute-start | bytes 786440 | tf_op jit(solution)/shard_map/ppermute | solution.py:188
  130.2 7.5 %collective-permute-start.7 = (f32[2,256,128]{2,1,0:T(8,128)}, f32[2,256,128]{2,1,0:T(8,128)S(1)}, u32[]{:S(2)}, u32[]{:S(2)}) collective-permute-start(f32[2,256,128]{2,1,0:T(8,128)} %get-tuple-element.35.refs_0_), channel_id=1, source_target_pairs={{0,128},{128,0},{1,129},{129,1},{2,130},{130,2},{3,131},{131,3},{4... | collective-permute-start | bytes 786440 | tf_op jit(solution)/shard_map/ppermute | solution.py:436
  130.2 8.0 %collective-permute-start.8 = (f32[2,256,128]{2,1,0:T(8,128)S(1)}, f32[2,256,128]{2,1,0:T(8,128)S(1)}, u32[]{:S(2)}, u32[]{:S(2)}) collective-permute-start(f32[2,256,128]{2,1,0:T(8,128)S(1)} %collective-permute-done.refs_1_), channel_id=1, source_target_pairs={{0,128},{128,0},{1,129},{129,1},{2,130},{130,2},{3,131},{131,3},{4... | collective-permute-start | bytes 786440 | tf_op jit(solution)/shard_map/ppermute | solution.py:436
  130.8 7.8 %collective-permute-start.9 = (f32[2,256,128]{2,1,0:T(8,128)S(1)}, f32[2,256,128]{2,1,0:T(8,128)S(1)}, u32[]{:S(2)}, u32[]{:S(2)}) collective-permute-start(f32[2,256,128]{2,1,0:T(8,128)S(1)} %collective-permute-done.1.refs_2_), channel_id=1, source_target_pairs={{0,128},{128,0},{1,129},{129,1},{2,130},{130,2},{3,131},{131,3},{4... | collective-permute-start | bytes 786440 | tf_op jit(solution)/shard_map/ppermute | solution.py:436
  154.6 135.8 %all-to-all-start.2 = ((f32[8,256,128]{2,1,0:T(8,128)}), f32[8,256,128]{2,1,0:T(8,128)S(1)}, u32[]{:S(2)}, u32[]{:S(2)}) async-start(f32[8,256,128]{2,1,0:T(8,128)} %get-tuple-element.63), calls=%async_computation.2 | async-start | bytes 2097152 | tf_op jit(solution)/shard_map/all_to_all | solution.py:438
  162.0 25.8 %collective-permute-start.15 = (f32[1,256,128]{2,1,0:T(8,128)}, f32[1,256,128]{2,1,0:T(8,128)S(1)}, u32[]{:S(2)}, u32[]{:S(2)}) collective-permute-start(f32[1,256,128]{2,1,0:T(8,128)} %get-tuple-element.45), channel_id=1, source_target_pairs={{0,112},{16,0},{32,16},{48,32},{64,48},{80,64},{96,80},{112,96},{1... | collective-permute-start | bytes 393224 | tf_op jit(solution)/shard_map/ppermute | solution.py:188
  165.1 31.2 %collective-permute-start.16 = (f32[1,256,128]{2,1,0:T(8,128)}, f32[1,256,128]{2,1,0:T(8,128)S(1)}, u32[]{:S(2)}, u32[]{:S(2)}) collective-permute-start(f32[1,256,128]{2,1,0:T(8,128)} %get-tuple-element.46), channel_id=1, source_target_pairs={{0,96},{16,112},{32,0},{48,16},{64,32},{80,48},{96,64},{112,80},{1... | collective-permute-start | bytes 393224 | tf_op jit(solution)/shard_map/ppermute | solution.py:188
  167.5 34.7 %collective-permute-start.17 = (f32[1,256,128]{2,1,0:T(8,128)}, f32[1,256,128]{2,1,0:T(8,128)S(1)}, u32[]{:S(2)}, u32[]{:S(2)}) collective-permute-start(f32[1,256,128]{2,1,0:T(8,128)} %get-tuple-element.47), channel_id=1, source_target_pairs={{0,80},{16,96},{32,112},{48,0},{64,16},{80,32},{96,48},{112,64},{1... | collective-permute-start | bytes 393224 | tf_op jit(solution)/shard_map/ppermute | solution.py:188
  168.9 33.3 %collective-permute-start.18 = (f32[1,256,128]{2,1,0:T(8,128)}, f32[1,256,128]{2,1,0:T(8,128)}, u32[]{:S(2)}, u32[]{:S(2)}) collective-permute-start(f32[1,256,128]{2,1,0:T(8,128)} %get-tuple-element.48), channel_id=1, source_target_pairs={{0,64},{16,80},{32,96},{48,112},{64,0},{80,16},{96,32},{112,48},{1... | collective-permute-start | bytes 393224 | tf_op jit(solution)/shard_map/ppermute | solution.py:188
  172.5 29.7 %collective-permute-start.19 = (f32[1,256,128]{2,1,0:T(8,128)}, f32[1,256,128]{2,1,0:T(8,128)}, u32[]{:S(2)}, u32[]{:S(2)}) collective-permute-start(f32[1,256,128]{2,1,0:T(8,128)} %get-tuple-element.49), channel_id=1, source_target_pairs={{0,48},{16,64},{32,80},{48,96},{64,112},{80,0},{96,16},{112,32},{1... | collective-permute-start | bytes 393224 | tf_op jit(solution)/shard_map/ppermute | solution.py:188
  187.7 18.0 %collective-permute-start.20 = (f32[1,256,128]{2,1,0:T(8,128)}, f32[1,256,128]{2,1,0:T(8,128)}, u32[]{:S(2)}, u32[]{:S(2)}) collective-permute-start(f32[1,256,128]{2,1,0:T(8,128)} %get-tuple-element.50), channel_id=1, source_target_pairs={{0,32},{16,48},{32,64},{48,80},{64,96},{80,112},{96,0},{112,16},{1... | collective-permute-start | bytes 393224 | tf_op jit(solution)/shard_map/ppermute | solution.py:188
  196.3 11.0 %collective-permute-start.21 = (f32[1,256,128]{2,1,0:T(8,128)}, f32[1,256,128]{2,1,0:T(8,128)}, u32[]{:S(2)}, u32[]{:S(2)}) collective-permute-start(f32[1,256,128]{2,1,0:T(8,128)} %get-tuple-element.51), channel_id=1, source_target_pairs={{0,16},{16,32},{32,48},{48,64},{64,80},{80,96},{96,112},{112,0},{1... | collective-permute-start | bytes 393224 | tf_op jit(solution)/shard_map/ppermute | solution.py:188
  218.8 12.2 %collective-permute-start.22 = (f32[1,256,128]{2,1,0:T(8,128)}, f32[1,256,128]{2,1,0:T(8,128)S(1)}, u32[]{:S(2)}, u32[]{:S(2)}) collective-permute-start(f32[1,256,128]{2,1,0:T(8,128)} %get-tuple-element.53), channel_id=1, source_target_pairs={{0,112},{16,0},{32,16},{48,32},{64,48},{80,64},{96,80},{112,96},{1... | collective-permute-start | bytes 393224 | tf_op jit(solution)/shard_map/ppermute | solution.py:188
  220.4 18.3 %collective-permute-start.23 = (f32[1,256,128]{2,1,0:T(8,128)}, f32[1,256,128]{2,1,0:T(8,128)S(1)}, u32[]{:S(2)}, u32[]{:S(2)}) collective-permute-start(f32[1,256,128]{2,1,0:T(8,128)} %get-tuple-element.54), channel_id=1, source_target_pairs={{0,96},{16,112},{32,0},{48,16},{64,32},{80,48},{96,64},{112,80},{1... | collective-permute-start | bytes 393224 | tf_op jit(solution)/shard_map/ppermute | solution.py:188
  222.8 18.2 %collective-permute-start.24 = (f32[1,256,128]{2,1,0:T(8,128)}, f32[1,256,128]{2,1,0:T(8,128)S(1)}, u32[]{:S(2)}, u32[]{:S(2)}) collective-permute-start(f32[1,256,128]{2,1,0:T(8,128)} %get-tuple-element.55), channel_id=1, source_target_pairs={{0,80},{16,96},{32,112},{48,0},{64,16},{80,32},{96,48},{112,64},{1... | collective-permute-start | bytes 393224 | tf_op jit(solution)/shard_map/ppermute | solution.py:188
  223.9 17.0 %collective-permute-start.25 = (f32[1,256,128]{2,1,0:T(8,128)}, f32[1,256,128]{2,1,0:T(8,128)S(1)}, u32[]{:S(2)}, u32[]{:S(2)}) collective-permute-start(f32[1,256,128]{2,1,0:T(8,128)} %get-tuple-element.56), channel_id=1, source_target_pairs={{0,64},{16,80},{32,96},{48,112},{64,0},{80,16},{96,32},{112,48},{1... | collective-permute-start | bytes 393224 | tf_op jit(solution)/shard_map/ppermute | solution.py:188
  227.7 18.6 %collective-permute-start.26 = (f32[1,256,128]{2,1,0:T(8,128)}, f32[1,256,128]{2,1,0:T(8,128)S(1)}, u32[]{:S(2)}, u32[]{:S(2)}) collective-permute-start(f32[1,256,128]{2,1,0:T(8,128)} %get-tuple-element.57), channel_id=1, source_target_pairs={{0,48},{16,64},{32,80},{48,96},{64,112},{80,0},{96,16},{112,32},{1... | collective-permute-start | bytes 393224 | tf_op jit(solution)/shard_map/ppermute | solution.py:188
  231.0 16.4 %collective-permute-start.27 = (f32[1,256,128]{2,1,0:T(8,128)}, f32[1,256,128]{2,1,0:T(8,128)S(1)}, u32[]{:S(2)}, u32[]{:S(2)}) collective-permute-start(f32[1,256,128]{2,1,0:T(8,128)} %get-tuple-element.58), channel_id=1, source_target_pairs={{0,32},{16,48},{32,64},{48,80},{64,96},{80,112},{96,0},{112,16},{1... | collective-permute-start | bytes 393224 | tf_op jit(solution)/shard_map/ppermute | solution.py:188
  238.7 12.8 %collective-permute-start.28 = (f32[1,256,128]{2,1,0:T(8,128)}, f32[1,256,128]{2,1,0:T(8,128)S(1)}, u32[]{:S(2)}, u32[]{:S(2)}) collective-permute-start(f32[1,256,128]{2,1,0:T(8,128)} %get-tuple-element.59), channel_id=1, source_target_pairs={{0,16},{16,32},{32,48},{48,64},{64,80},{80,96},{96,112},{112,0},{1... | collective-permute-start | bytes 393224 | tf_op jit(solution)/shard_map/ppermute | solution.py:188
  262.6 7.5 %collective-permute-start.33 = (f32[8,128]{1,0:T(8,128)S(1)}, f32[8,128]{1,0:T(8,128)S(1)}, u32[]{:S(2)}, u32[]{:S(2)}) collective-permute-start(f32[8,128]{1,0:T(8,128)S(1)} %add_add_fusion.3), channel_id=1, source_target_pairs={{0,32},{16,48},{32,64},{48,80},{64,96},{80,112},{96,0},{112,16},{1... | collective-permute-start | bytes 12296 | tf_op jit(solution)/shard_map/ppermute | solution.py:463
  263.9 6.2 %collective-permute-start.34 = (f32[8,128]{1,0:T(8,128)S(1)}, f32[8,128]{1,0:T(8,128)S(1)}, u32[]{:S(2)}, u32[]{:S(2)}) collective-permute-start(f32[8,128]{1,0:T(8,128)S(1)} %add_add_fusion.3), channel_id=1, source_target_pairs={{0,96},{16,112},{32,0},{48,16},{64,32},{80,48},{96,64},{112,80},{1... | collective-permute-start | bytes 12296 | tf_op jit(solution)/shard_map/ppermute | solution.py:463
  266.8 7.5 %collective-permute-start.32 = (f32[8,128]{1,0:T(8,128)S(1)}, f32[8,128]{1,0:T(8,128)S(1)}, u32[]{:S(2)}, u32[]{:S(2)}) collective-permute-start(f32[8,128]{1,0:T(8,128)S(1)} %add_add_fusion.3), channel_id=1, source_target_pairs={{0,64},{16,80},{32,96},{48,112},{64,0},{80,16},{96,32},{112,48},{1... | collective-permute-start | bytes 12296 | tf_op jit(solution)/shard_map/ppermute | solution.py:463
  276.3 5.1 %collective-permute-start.35 = (f32[8,128]{1,0:T(8,128)S(1)}, f32[8,128]{1,0:T(8,128)S(1)}, u32[]{:S(2)}, u32[]{:S(2)}) collective-permute-start(f32[8,128]{1,0:T(8,128)S(1)} %add_add_fusion.2), channel_id=1, source_target_pairs={{0,2},{1,3},{2,0},{3,1},{4,6},{5,7},{6,4},{7,5},{8,10},{9,11},{10,... | collective-permute-start | bytes 12296 | tf_op jit(solution)/shard_map/ppermute | solution.py:463
  284.7 5.1 %collective-permute-start.38 = (f32[8,128]{1,0:T(8,128)S(1)}, f32[8,128]{1,0:T(8,128)S(1)}, u32[]{:S(2)}, u32[]{:S(2)}) collective-permute-start(f32[8,128]{1,0:T(8,128)S(1)} %add_add_fusion.1), channel_id=1, source_target_pairs={{0,8},{4,12},{8,0},{12,4},{1,9},{5,13},{9,1},{13,5},{2,10},{6,14},... | collective-permute-start | bytes 12296 | tf_op jit(solution)/shard_map/ppermute | solution.py:463
  (40 other events, 328.4 us)

commit v2 on v1

--- a/solution.py
+++ b/solution.py
@@ -21,26 +21,25 @@
 HIGH = lax.Precision.HIGHEST
 
 
-def toeplitz_parts():
-    lags = np.arange(M)[:, None] - np.arange(M)[None, :]
-    off = lags != 0
-    base = np.zeros((M, M))
-    base[off] = (1.0 / 16) * (math.pi / M) * (-1.0) ** lags[off] / np.sin(math.pi * lags[off] / M)
+def turns():
     turn = 2.0 * math.pi / N * (np.arange(16) - 8)[:, None] * np.arange(M)[None, :]
-    cos_r, sin_r = np.cos(turn), np.sin(turn)
-    cos_c = np.zeros((M, 128))
-    sin_c = np.zeros((M, 128))
-    cos_c[:, :16] = cos_r.T
-    sin_c[:, :16] = sin_r.T
-    return [np.asarray(a, np.float32) for a in (base, cos_r, sin_r, cos_c, sin_c)]
-
-
-def table_kernel(base, cos_r, sin_r, cos_c, sin_c, out):
+    tall = np.zeros((2, M, 128), np.float32)
+    tall[0, :, :16] = np.cos(turn).T
+    tall[1, :, :16] = np.sin(turn).T
+    return np.stack([np.cos(turn), np.sin(turn)]).astype(np.float32), tall
+
+
+def table_kernel(wide, tall, out, base):
     left = lax.broadcasted_iota(jnp.int32, (M, M), 0)
     right = lax.broadcasted_iota(jnp.int32, (M, M), 1)
+    lag = left - right
+    size = jnp.abs(lag)
+    angle = jnp.minimum(size, M - size).astype(jnp.float32) * (math.pi / M)
+    scale = jnp.where((lag > 0) == (lax.rem(size, 2) == 0), math.pi / (16 * M), -math.pi / (16 * M))
+    base[...] = jnp.where(lag == 0, 0.0, scale / jnp.where(lag == 0, 1.0, jnp.sin(angle)))
     for k in range(9):
-        ca, sa = cos_c[:, k : k + 1], sin_c[:, k : k + 1]
-        cb, sb = cos_r[k : k + 1, :], sin_r[k : k + 1, :]
+        ca, sa = tall[0, :, k : k + 1], tall[1, :, k : k + 1]
+        cb, sb = wide[0, k : k + 1, :], wide[1, k : k + 1, :]
         out[k] = base[...] * (ca * cb + sa * sb)
         if 0 < k < 8:
             middle = 2.0 * math.pi / N * (k - 8) / 16
@@ -190,17 +189,15 @@
 
 
 def spectral_x(table, spec, res):
-    res[0, :, :128] = jnp.dot(table[0], spec[0, :, :128], precision=HIGH)
-    res[0, :, 128:] = jnp.dot(table[8], spec[0, :, 128:], precision=HIGH)
-
     def body(k, carry):
+        lone = k == 0
         a = jnp.dot(table[k], spec[k], precision=HIGH)
         b = jnp.dot(table[8 + k], spec[k], precision=HIGH)
-        res[k, :, :128] = a[:, :128] - b[:, 128:]
-        res[k, :, 128:] = a[:, 128:] + b[:, :128]
-        return carry
-
-    lax.fori_loop(1, 8, body, 0)
+        res[k, :, :128] = a[:, :128] - jnp.where(lone, 0.0, b[:, 128:])
+        res[k, :, 128:] = jnp.where(lone, b[:, 128:], a[:, 128:] + b[:, :128])
+        return carry
+
+    lax.fori_loop(0, 8, body, 0)
 
 
 STEP = 16
@@ -251,8 +248,29 @@
     return vmem_call(grad_v_kernel, [f32(1, 256, 128)] * 8, X_SCRATCH)(table, *blocks)
 
 
+def stack_first_kernel(*refs):
+    blocks, out, sems = refs[:8], refs[8], refs[9]
+    copies = [pltpu.make_async_copy(blocks[j].at[0], out.at[j], sems.at[j]) for j in range(8)]
+    for copy in copies:
+        copy.start()
+    for copy in copies:
+        copy.wait()
+
+
+def stack_first(blocks):
+    anywhere = pl.BlockSpec(memory_space=pl.ANY)
+    return pl.pallas_call(
+        stack_first_kernel,
+        out_shape=f32(8, 256, 128),
+        in_specs=[anywhere] * 8,
+        out_specs=anywhere,
+        scratch_shapes=[pltpu.SemaphoreType.DMA((8,))],
+        name="stack_first",
+    )(*blocks)
+
+
 def grad_uw_kernel(row, table, *refs):
-    blocks, other, out, sums, spec, res = refs[:8], refs[8:16], refs[16], refs[17], refs[18], refs[19]
+    blocks, other, out, sums, spec, res = refs[:8], *refs[8:]
     lane = lane_ids(STEP)
     low = lane < 64
     first = lax.rem(lane // 32, 2) == 0
@@ -277,7 +295,7 @@
             a, b = values[2 * j], values[2 * j + 1]
             u_x = jnp.where(low, a, pltpu.roll(b, 64, 1))
             w_x = jnp.where(low, pltpu.roll(a, 64, 1), b)
-            diff = blocks[j][0, rows, :] - other[j][0, rows, :]
+            diff = blocks[j][0, rows, :] - other[j, rows, :]
             u_z = 0.5 * jnp.where(first, pltpu.roll(diff, 96, 1), -pltpu.roll(diff, 32, 1))
             cross = u_z + w_x
             part = u_x * u_x + 0.5 * (cross * cross)
@@ -293,7 +311,7 @@
 
 def grad_uw(row, table, other, blocks):
     outs = [f32(8, 256, 128), f32(8, 128)]
-    return vmem_call(grad_uw_kernel, outs, X_SCRATCH, smem=1)(row, table, *blocks, *other)
+    return vmem_call(grad_uw_kernel, outs, X_SCRATCH, smem=1)(row, table, *blocks, other)
 
 
 def grad_y_kernel(table, data, out, spec, res):
@@ -311,17 +329,16 @@
         return carry
 
     lax.fori_loop(0, 48, forward, 0)
-    res[0, :192] = jnp.dot(spec[0, :192], table[0], precision=HIGH) * -1.0
-    res[0, 192:] = jnp.dot(spec[0, 192:], table[8], precision=HIGH) * -1.0
 
     def middle(f, carry):
+        lone = f == 0
         a = jnp.dot(spec[f], table[f], precision=HIGH)
         b = jnp.dot(spec[f], table[8 + f], precision=HIGH)
-        res[f, :192] = -a[:192] - b[192:]
-        res[f, 192:] = b[:192] - a[192:]
-        return carry
-
-    lax.fori_loop(1, 8, middle, 0)
+        res[f, :192] = -a[:192] - jnp.where(lone, 0.0, b[192:])
+        res[f, 192:] = jnp.where(lone, -b[192:], b[:192] - a[192:])
+        return carry
+
+    lax.fori_loop(0, 8, middle, 0)
 
     def backward(i, carry):
         k = i // 4
@@ -394,7 +411,7 @@
     boxes[...] = jnp.where(mine, found * (1.0 / (4 * COARSE * COARSE)), zero)
 
 
-def final_kernel(part, select, held, out, boxes, lines):
+def final_kernel(part, held, out, boxes, lines):
 
     def body(a, carry):
         rows = pl.ds(pl.multiple_of(a * 32, 32), 32)
@@ -412,28 +429,31 @@
         return carry
 
     lax.fori_loop(0, 8, body, 0)
-    boxes[...] = jnp.dot(jnp.sum(lines[...], axis=1), select[...], precision=HIGH)
+    cell = lax.broadcasted_iota(jnp.int32, (256, 128), 0) // FINE
+    select = jnp.where(cell == lax.broadcasted_iota(jnp.int32, (256, 128), 1), 1.0 / (4 * FINE * FINE), 0.0)
+    boxes[...] = jnp.dot(jnp.sum(lines[...], axis=1), select, precision=HIGH)
 
 
 def whole_step(velocity):
     row = lax.axis_index("row")
     col = lax.axis_index(COL)
     row_arg = row.astype(jnp.int32).reshape(1)
-    parts = [jnp.asarray(a) for a in toeplitz_parts()]
+    parts = [jnp.asarray(a) for a in turns()]
     for_cols = vmem_call(pack_cols_kernel, f32(32, 3, 2, 16, 256))(velocity)
     lines = lax.all_to_all(for_cols, PLANE_COL, split_axis=0, concat_axis=0, tiled=True)
     v_blocks = pack_rows(row_arg, velocity, (1,))
     v_blocks = send_blocks(v_blocks)
     uw_blocks = pack_rows(row_arg, velocity, (0, 2))
     uw_blocks = send_blocks(uw_blocks)
-    table = vmem_call(table_kernel, f32(16, M, M))(*parts)
+    table = vmem_call(table_kernel, f32(16, M, M), (pltpu.VMEM((M, M), jnp.float32),))(*parts)
     v_x = grad_v(table, v_blocks)
     v_x = send_blocks(v_x)
     y_terms = grad_y(table, lines.reshape(2, 16, 3, 2, 16, 256))
     y_terms = lax.all_to_all(
         y_terms.reshape(32, 2, 2, 16, 256), PLANE_COL, split_axis=0, concat_axis=0, tiled=True
     )
-    other = [lax.ppermute(b, "plane", [(0, 1), (1, 0)]) for b in uw_blocks]
+    other = stack_first(uw_blocks)
+    other = lax.ppermute(other, "plane", [(0, 1), (1, 0)])
     x_terms, x_sums = grad_uw(row_arg, table, other, uw_blocks)
     x_terms = lax.all_to_all(x_terms, "row", split_axis=0, concat_axis=0, tiled=True)
     held = pltpu.VMEM((ROWS, 256, 128), jnp.float32)
@@ -441,19 +461,16 @@
     part, coarse = vmem_call(partial_kernel, [f32(2, 512, 256), f32(8, 128)], (held,), smem=1)(
         place, y_terms, x_sums, *v_x
     )
+    coarse = sum_of_four(coarse, "col_1", lambda i, n: (i + (2, 1, 3)[n]) % 4)
+    coarse = sum_of_four(coarse, "col_0", lambda i, n: (i + (2, 1, 3)[n]) % 4)
     coarse = sum_of_four(coarse, ("plane", "row"), lambda i, n: i ^ (8, 1, 9)[n])
     coarse = sum_of_four(coarse, "row", lambda i, n: (i + (4, 2, 6)[n]) % 8)
-    coarse = sum_of_four(coarse, "col_1", lambda i, n: (i + (2, 1, 3)[n]) % 4)
-    coarse = sum_of_four(coarse, "col_0", lambda i, n: (i + (2, 1, 3)[n]) % 4)
     coarse = coarse[:4, :4]
-    select = np.zeros((256, 128), np.float32)
-    select[np.arange(256), np.arange(256) // FINE] = 1.0 / (4 * FINE * FINE)
-    coarse, part = lax.optimization_barrier((coarse, part))
     dissip, fine = vmem_call(
         final_kernel,
         [f32(2, 512, 256), f32(16, 128)],
         (pltpu.VMEM((16, 8, 256), jnp.float32),),
-    )(part, jnp.asarray(select), x_terms)
+    )(part, x_terms)
     fine = (fine + lax.ppermute(fine, "plane", [(0, 1), (1, 0)]))[:, :8]
     return dissip, fine, coarse
 

time: 301 us -> 329 us (1.093)
  Pallas kernels: 65.8 us -> 99.4 us
  waiting for transfers between devices: 148 us -> 144 us
    pallas_call x0 -> x1, Pallas kernels: none -> 32.9 us  [stack_first(): pl.pallas_call(stack_first_kernel, out_shape=f32(8, 256, 128), in_specs=[...]
    ppermute x12, waiting for transfers between devices: 12.7 us -> 9 us  [sum_of_four(): lax.ppermute(values, axis, [(i, partner(i, n)) for i in range(size)])]
  transfers between devices with their start and end apart: 45 -> 38, of which waited for: 26 -> 22; matrix products, arithmetic and copies ran while one was open for 1% -> 1% of each run, Pallas kernels for 15% -> 25%
where the time goes in v2:
time: 329 us; the launch traced here: 327 us
  waiting for transfers between devices  144 us (44%)
  Pallas kernels  99.4 us (30%)
  starting transfers between devices  75.3 us (23%)
  local copies, waits for them, and re-layouts  5.51 us (2%)
    ppermute x21, waiting for transfers between devices, send_blocks(): got[(ROWS - dist) % ROWS] = lax.ppermute(blocks[dist], 'row', perm)  98 us
    pallas_call x7, Pallas kernels, call(): pl.pallas_call(kernel, out_shape=list(outs) if many else outs, in_specs=s...  57.4 us
    ppermute x21, starting transfers between devices, send_blocks(): got[(ROWS - dist) % ROWS] = lax.ppermute(blocks[dist], 'row', perm)  38.3 us
    all_to_all x1, waiting for transfers between devices, whole_step(): lax.all_to_all(for_cols, PLANE_COL, split_axis=0, concat_axis=0, tiled=True)  34.2 us
    pallas_call x1, Pallas kernels, stack_first(): pl.pallas_call(stack_first_kernel, out_shape=f32(8, 256, 128), in_specs=[...  32.9 us
    ppermute x12, starting transfers between devices, sum_of_four(): lax.ppermute(values, axis, [(i, partner(i, n)) for i in range(size)])  19.2 us
    pallas_call x2, Pallas kernels, pack_rows(): pl.pallas_call(functools.partial(pack_rows_kernel, count=count), out_shap...  9.12 us
    ppermute x12, waiting for transfers between devices, sum_of_four(): lax.ppermute(values, axis, [(i, partner(i, n)) for i in range(size)])  9 us
  transfers between devices with their start and end apart: 38, of which 22 were waited for; matrix products, arithmetic and copies ran while one was open for 1% of the time, Pallas kernels for 25%

profile of v2, /device:TPU:2, one launch (start us, length us, event | category | flops | bytes accessed | tf_op | source)
XLA Modules:
  0.0 327.2 jit_solution(529014239863254732)
XLA Ops:
  0.6 3.8 %shard_map.59 = f32[32,3,2,16,256]{4,3,2,1,0:T(8,128)} custom-call(f32[3,2,512,256]{3,2,1,0:T(8,128)} %refs_0_.3), custom_call_target="tpu_custom_call" | custom-call | tf_op jit(solution)/shard_map/pallas_call | solution.py:55
  4.5 7.6 %all-to-all-start = ((f32[32,3,2,16,256]{4,3,2,1,0:T(8,128)}), f32[32,3,2,16,256]{4,3,2,1,0:T(8,128)S(1)}, u32[]{:S(2)}, u32[]{:S(2)}) async-start(f32[32,3,2,16,256]{4,3,2,1,0:T(8,128)} %shard_map.59), calls=%async_computation | async-start | bytes 6291456 | tf_op jit(solution)/shard_map/all_to_all | solution.py:443
  12.1 4.7 %shard_map.58.table = f32[16,256,256]{2,1,0:T(8,128)} custom-call(f32[2,16,256]{2,1,0:T(8,128)} %constant.19.clone.wide, f32[2,256,128]{2,1,0:T(8,128)} %constant.20.clone.tall), custom_call_target="tpu_custom_call" | custom-call | tf_op jit(solution)/shard_map/pallas_call | solution.py:55
  16.8 34.2 %all-to-all-done = f32[32,3,2,16,256]{4,3,2,1,0:T(8,128)S(1)} async-done(((f32[32,3,2,16,256]{4,3,2,1,0:T(8,128)}), f32[32,3,2,16,256]{4,3,2,1,0:T(8,128)S(1)}, u32[]{:S(2)}, u32[]{:S(2)}) %all-to-all-start) | async-done | bytes 3145760 | tf_op jit(solution)/shard_map/all_to_all | solution.py:443
  52.7 14.5 %shard_map.60 = f32[2,16,2,2,16,256]{5,4,3,2,1,0:T(8,128)} custom-call(f32[16,256,256]{2,1,0:T(8,128)} %shard_map.58.table, f32[2,16,3,2,16,256]{5,4,3,2,1,0:T(8,128)} %bitcast.4), custom_call_target="tpu_custom_call" | custom-call | tf_op jit(solution)/shard_map/pallas_call | solution.py:55
  67.2 6.5 %all-to-all-start.1 = ((f32[32,2,2,16,256]{4,3,2,1,0:T(8,128)}), f32[32,2,2,16,256]{4,3,2,1,0:T(8,128)S(1)}, u32[]{:S(2)}, u32[]{:S(2)}) async-start(f32[32,2,2,16,256]{4,3,2,1,0:T(8,128)} %bitcast.5), calls=%async_computation.1 | async-start | bytes 4194304 | tf_op jit(solution)/shard_map/all_to_all | solution.py:452
  73.8 5.3 %pack_rows.2 = (f32[2,256,128]{2,1,0:T(8,128)}, f32[2,256,128]{2,1,0:T(8,128)}, f32[2,256,128]{2,1,0:T(8,128)}, f32[2,256,128]{2,1,0:T(8,128)}, f32[2,256,128]{2...) custom-call(s32[1]{0:T(128)} %bitcast.row, f32[3,2,512,256]{3,2,1,0:T(8,128)} %refs_0_.3, ...), custom_call_target="tpu_custom_call" | custom-call | tf_op jit(solution)/shard_map/pack_rows/pallas_call | solution.py:162
  79.1 5.9 %collective-permute-start = (f32[2,256,128]{2,1,0:T(8,128)}, f32[2,256,128]{2,1,0:T(8,128)S(1)}, u32[]{:S(2)}, u32[]{:S(2)}) collective-permute-start(f32[2,256,128]{2,1,0:T(8,128)} %get-tuple-element.34), channel_id=1, source_target_pairs={{0,112},{16,0},{32,16},{48,32},{64,48},{80,64},{96,80},{112,96},{1... | collective-permute-start | bytes 786440 | tf_op jit(solution)/shard_map/ppermute | solution.py:187
  86.9 5.0 %collective-permute-start.3 = (f32[2,256,128]{2,1,0:T(8,128)}, f32[2,256,128]{2,1,0:T(8,128)S(1)}, u32[]{:S(2)}, u32[]{:S(2)}) collective-permute-start(f32[2,256,128]{2,1,0:T(8,128)} %get-tuple-element.37), channel_id=1, source_target_pairs={{0,64},{16,80},{32,96},{48,112},{64,0},{80,16},{96,32},{112,48},{1... | collective-permute-start | bytes 786440 | tf_op jit(solution)/shard_map/ppermute | solution.py:187
  91.9 6.8 %collective-permute-done.refs_1_ = f32[2,256,128]{2,1,0:T(8,128)S(1)} collective-permute-done((f32[2,256,128]{2,1,0:T(8,128)}, f32[2,256,128]{2,1,0:T(8,128)S(1)}, u32[]{:S(2)}, u32[]{:S(2)}) %collective-permute-start) | collective-permute-done | bytes 262176 | tf_op jit(solution)/shard_map/ppermute | solution.py:187
  98.7 12.8 %collective-permute-done.1.refs_2_ = f32[2,256,128]{2,1,0:T(8,128)S(1)} collective-permute-done((f32[2,256,128]{2,1,0:T(8,128)}, f32[2,256,128]{2,1,0:T(8,128)S(1)}, u32[]{:S(2)}, u32[]{:S(2)}) %collective-permute-start.1) | collective-permute-done | bytes 262176 | tf_op jit(solution)/shard_map/ppermute | solution.py:187
  111.5 19.0 %collective-permute-done.2.refs_3_ = f32[2,256,128]{2,1,0:T(8,128)S(1)} collective-permute-done((f32[2,256,128]{2,1,0:T(8,128)}, f32[2,256,128]{2,1,0:T(8,128)S(1)}, u32[]{:S(2)}, u32[]{:S(2)}) %collective-permute-start.2) | collective-permute-done | bytes 262176 | tf_op jit(solution)/shard_map/ppermute | solution.py:187
  130.5 4.0 %collective-permute-done.5.refs_6_ = f32[2,256,128]{2,1,0:T(8,128)} collective-permute-done((f32[2,256,128]{2,1,0:T(8,128)}, f32[2,256,128]{2,1,0:T(8,128)}, u32[]{:S(2)}, u32[]{:S(2)}) %collective-permute-start.5) | collective-permute-done | bytes 262176 | tf_op jit(solution)/shard_map/ppermute | solution.py:187
  134.4 3.6 %collective-permute-done.6.refs_7_ = f32[2,256,128]{2,1,0:T(8,128)} collective-permute-done((f32[2,256,128]{2,1,0:T(8,128)}, f32[2,256,128]{2,1,0:T(8,128)}, u32[]{:S(2)}, u32[]{:S(2)}) %collective-permute-start.6) | collective-permute-done | bytes 262176 | tf_op jit(solution)/shard_map/ppermute | solution.py:187
  138.1 32.9 %stack_first.1 = f32[8,256,128]{2,1,0:T(8,128)} custom-call(f32[2,256,128]{2,1,0:T(8,128)} %get-tuple-element.33.refs_0_, f32[2,256,128]{2,1,0:T(8,128)} %copy-done.4, f32[2,256,128]{2,1,0:T(8,128)} %copy-done.5, f32[2,256,128]{2,1,0:T(8,128)} %copy-done.6, f32[2,256,128]{2,1,0:T(8,128)} %copy-done.7, f32[2,256,128]{2,1,0:T(8,128)} %copy-done.8, ...), custom_call_target="tpu_custom_call" | custom-call | tf_op jit(solution)/shard_map/stack_first/pallas_call | solution.py:262
  175.0 13.2 %shard_map.61 = (f32[8,256,128]{2,1,0:T(8,128)}, f32[8,128]{1,0:T(8,128)}) custom-call(s32[1]{0:T(128)} %bitcast.row, f32[16,256,256]{2,1,0:T(8,128)} %shard_map.58.table, f32[2,256,128]{2,1,0:T(8,128)} %get-tuple-element.33.refs_0_, f32[2,256,128]{2,1,0:T(8,128)} %copy-done.4, f32[2,256,128]{2,1,0:T(8,128)} %copy-done.5, f32[2,256,128]{2,1,0:T(8,128)} %copy-done.6, ...), custom_call_target="tpu_custom_call" | custom-call | tf_op jit(solution)/shard_map/pallas_call | solution.py:55
  188.2 3.6 %all-to-all-start.2 = ((f32[8,256,128]{2,1,0:T(8,128)}), f32[8,256,128]{2,1,0:T(8,128)S(1)}, u32[]{:S(2)}, u32[]{:S(2)}) async-start(f32[8,256,128]{2,1,0:T(8,128)} %get-tuple-element.59), calls=%async_computation.2 | async-start | bytes 2097152 | tf_op jit(solution)/shard_map/all_to_all | solution.py:458
  191.8 3.8 %pack_rows.3 = (f32[1,256,128]{2,1,0:T(8,128)}, f32[1,256,128]{2,1,0:T(8,128)}, f32[1,256,128]{2,1,0:T(8,128)}, f32[1,256,128]{2,1,0:T(8,128)}, f32[1,256,128]{2...) custom-call(s32[1]{0:T(128)} %bitcast.row, f32[3,2,512,256]{3,2,1,0:T(8,128)} %refs_0_.3), custom_call_target="tpu_custom_call" | custom-call | tf_op jit(solution)/shard_map/pack_rows/pallas_call | solution.py:162
  202.5 3.6 %collective-permute-start.11 = (f32[1,256,128]{2,1,0:T(8,128)}, f32[1,256,128]{2,1,0:T(8,128)}, u32[]{:S(2)}, u32[]{:S(2)}) collective-permute-start(f32[1,256,128]{2,1,0:T(8,128)} %get-tuple-element.46), channel_id=1, source_target_pairs={{0,64},{16,80},{32,96},{48,112},{64,0},{80,16},{96,32},{112,48},{1... | collective-permute-start | bytes 393224 | tf_op jit(solution)/shard_map/ppermute | solution.py:187
  206.4 15.1 %collective-permute-done.8.refs_1_ = f32[1,256,128]{2,1,0:T(8,128)S(1)} collective-permute-done((f32[1,256,128]{2,1,0:T(8,128)}, f32[1,256,128]{2,1,0:T(8,128)S(1)}, u32[]{:S(2)}, u32[]{:S(2)}) %collective-permute-start.8) | collective-permute-done | bytes 131104 | tf_op jit(solution)/shard_map/ppermute | solution.py:187
  223.1 6.9 %collective-permute-done.9.refs_2_ = f32[1,256,128]{2,1,0:T(8,128)S(1)} collective-permute-done((f32[1,256,128]{2,1,0:T(8,128)}, f32[1,256,128]{2,1,0:T(8,128)S(1)}, u32[]{:S(2)}, u32[]{:S(2)}) %collective-permute-start.9) | collective-permute-done | bytes 131104 | tf_op jit(solution)/shard_map/ppermute | solution.py:187
  230.0 5.8 %collective-permute-done.10.refs_3_ = f32[1,256,128]{2,1,0:T(8,128)S(1)} collective-permute-done((f32[1,256,128]{2,1,0:T(8,128)}, f32[1,256,128]{2,1,0:T(8,128)S(1)}, u32[]{:S(2)}, u32[]{:S(2)}) %collective-permute-start.10) | collective-permute-done | bytes 131104 | tf_op jit(solution)/shard_map/ppermute | solution.py:187
  235.9 3.6 %collective-permute-done.13.refs_6_ = f32[1,256,128]{2,1,0:T(8,128)} collective-permute-done((f32[1,256,128]{2,1,0:T(8,128)}, f32[1,256,128]{2,1,0:T(8,128)}, u32[]{:S(2)}, u32[]{:S(2)}) %collective-permute-start.13) | collective-permute-done | bytes 131104 | tf_op jit(solution)/shard_map/ppermute | solution.py:187
  240.9 11.5 %shard_map.62 = (f32[1,256,128]{2,1,0:T(8,128)}, f32[1,256,128]{2,1,0:T(8,128)}, f32[1,256,128]{2,1,0:T(8,128)}, f32[1,256,128]{2,1,0:T(8,128)}, f32[1,256,128]{...) custom-call(f32[16,256,256]{2,1,0:T(8,128)} %shard_map.58.table, ...), custom_call_target="tpu_custom_call" | custom-call | tf_op jit(solution)/shard_map/pallas_call | solution.py:55
  257.6 3.8 %collective-permute-start.18 = (f32[1,256,128]{2,1,0:T(8,128)}, f32[1,256,128]{2,1,0:T(8,128)S(1)}, u32[]{:S(2)}, u32[]{:S(2)}) collective-permute-start(f32[1,256,128]{2,1,0:T(8,128)} %get-tuple-element.54), channel_id=1, source_target_pairs={{0,64},{16,80},{32,96},{48,112},{64,0},{80,16},{96,32},{112,48},{1... | collective-permute-start | bytes 393224 | tf_op jit(solution)/shard_map/ppermute | solution.py:187
  261.4 3.3 %collective-permute-start.19 = (f32[1,256,128]{2,1,0:T(8,128)}, f32[1,256,128]{2,1,0:T(8,128)S(1)}, u32[]{:S(2)}, u32[]{:S(2)}) collective-permute-start(f32[1,256,128]{2,1,0:T(8,128)} %get-tuple-element.55), channel_id=1, source_target_pairs={{0,48},{16,64},{32,80},{48,96},{64,112},{80,0},{96,16},{112,32},{1... | collective-permute-start | bytes 393224 | tf_op jit(solution)/shard_map/ppermute | solution.py:187
  265.5 6.8 %collective-permute-done.16.refs_2_ = f32[1,256,128]{2,1,0:T(8,128)S(1)} collective-permute-done((f32[1,256,128]{2,1,0:T(8,128)}, f32[1,256,128]{2,1,0:T(8,128)S(1)}, u32[]{:S(2)}, u32[]{:S(2)}) %collective-permute-start.16) | collective-permute-done | bytes 131104 | tf_op jit(solution)/shard_map/ppermute | solution.py:187
  274.7 5.2 %collective-permute-done.19.refs_5_ = f32[1,256,128]{2,1,0:T(8,128)S(1)} collective-permute-done((f32[1,256,128]{2,1,0:T(8,128)}, f32[1,256,128]{2,1,0:T(8,128)S(1)}, u32[]{:S(2)}, u32[]{:S(2)}) %collective-permute-start.19) | collective-permute-done | bytes 131104 | tf_op jit(solution)/shard_map/ppermute | solution.py:187
  281.2 3.9 %collective-permute-done.21.refs_7_ = f32[1,256,128]{2,1,0:T(8,128)S(1)} collective-permute-done((f32[1,256,128]{2,1,0:T(8,128)}, f32[1,256,128]{2,1,0:T(8,128)S(1)}, u32[]{:S(2)}, u32[]{:S(2)}) %collective-permute-start.21) | collective-permute-done | bytes 131104 | tf_op jit(solution)/shard_map/ppermute | solution.py:187
  285.8 5.6 %shard_map.63 = (f32[2,512,256]{2,1,0:T(8,128)}, f32[8,128]{1,0:T(8,128)}) custom-call(s32[2]{0:T(128)} %pad_add_fusion.place, f32[32,2,2,16,256]{4,3,2,1,0:T(8,128)} %copy-done.1, f32[8,128]{1,0:T(8,128)} %get-tuple-element.41.x_sums, f32[1,256,128]{2,1,0:T(8,128)} %get-tuple-element.50.refs_0_, f32[1,256,128]{2,1,0:T(8,128)} %copy-done.12, ...), custom_call_target="tpu_custom_call" | custom-call | tf_op jit(solution)/shard_map/pallas_call | solution.py:55
  310.9 3.9 %shard_map.64 = (f32[2,512,256]{2,1,0:T(8,128)}, f32[16,128]{1,0:T(8,128)}) custom-call(f32[2,512,256]{2,1,0:T(8,128)} %get-tuple-element.58.part, f32[8,256,128]{2,1,0:T(8,128)} %copy-done.2), custom_call_target="tpu_custom_call" | custom-call | tf_op jit(solution)/shard_map/pallas_call | solution.py:55
  319.1 3.7 %collective-permute-start.32 = (f32[8,128]{1,0:T(8,128)S(1)}, f32[8,128]{1,0:T(8,128)S(1)}, u32[]{:S(2)}, u32[]{:S(2)}) collective-permute-start(f32[8,128]{1,0:T(8,128)S(1)} %add_add_fusion.1), channel_id=1, source_target_pairs={{0,64},{16,80},{32,96},{48,112},{64,0},{80,16},{96,32},{112,48},{1... | collective-permute-start | bytes 12296 | tf_op jit(solution)/shard_map/ppermute | solution.py:480
  (100 shorter events, 56.3 us)
Async XLA Ops:
  4.5 46.6 %all-to-all-start = ((f32[32,3,2,16,256]{4,3,2,1,0:T(8,128)}), f32[32,3,2,16,256]{4,3,2,1,0:T(8,128)S(1)}, u32[]{:S(2)}, u32[]{:S(2)}) async-start(f32[32,3,2,16,256]{4,3,2,1,0:T(8,128)} %shard_map.59), calls=%async_computation | async-start | bytes 6291456 | tf_op jit(solution)/shard_map/all_to_all | solution.py:443
  67.2 121.0 %all-to-all-start.1 = ((f32[32,2,2,16,256]{4,3,2,1,0:T(8,128)}), f32[32,2,2,16,256]{4,3,2,1,0:T(8,128)S(1)}, u32[]{:S(2)}, u32[]{:S(2)}) async-start(f32[32,2,2,16,256]{4,3,2,1,0:T(8,128)} %bitcast.5), calls=%async_computation.1 | async-start | bytes 4194304 | tf_op jit(solution)/shard_map/all_to_all | solution.py:452
  79.1 19.6 %collective-permute-start = (f32[2,256,128]{2,1,0:T(8,128)}, f32[2,256,128]{2,1,0:T(8,128)S(1)}, u32[]{:S(2)}, u32[]{:S(2)}) collective-permute-start(f32[2,256,128]{2,1,0:T(8,128)} %get-tuple-element.34), channel_id=1, source_target_pairs={{0,112},{16,0},{32,16},{48,32},{64,48},{80,64},{96,80},{112,96},{1... | collective-permute-start | bytes 786440 | tf_op jit(solution)/shard_map/ppermute | solution.py:187
  85.0 26.5 %collective-permute-start.1 = (f32[2,256,128]{2,1,0:T(8,128)}, f32[2,256,128]{2,1,0:T(8,128)S(1)}, u32[]{:S(2)}, u32[]{:S(2)}) collective-permute-start(f32[2,256,128]{2,1,0:T(8,128)} %get-tuple-element.35), channel_id=1, source_target_pairs={{0,96},{16,112},{32,0},{48,16},{64,32},{80,48},{96,64},{112,80},{1... | collective-permute-start | bytes 786440 | tf_op jit(solution)/shard_map/ppermute | solution.py:187
  86.4 44.0 %collective-permute-start.2 = (f32[2,256,128]{2,1,0:T(8,128)}, f32[2,256,128]{2,1,0:T(8,128)S(1)}, u32[]{:S(2)}, u32[]{:S(2)}) collective-permute-start(f32[2,256,128]{2,1,0:T(8,128)} %get-tuple-element.36), channel_id=1, source_target_pairs={{0,80},{16,96},{32,112},{48,0},{64,16},{80,32},{96,48},{112,64},{1... | collective-permute-start | bytes 786440 | tf_op jit(solution)/shard_map/ppermute | solution.py:187
  86.9 43.6 %collective-permute-start.3 = (f32[2,256,128]{2,1,0:T(8,128)}, f32[2,256,128]{2,1,0:T(8,128)S(1)}, u32[]{:S(2)}, u32[]{:S(2)}) collective-permute-start(f32[2,256,128]{2,1,0:T(8,128)} %get-tuple-element.37), channel_id=1, source_target_pairs={{0,64},{16,80},{32,96},{48,112},{64,0},{80,16},{96,32},{112,48},{1... | collective-permute-start | bytes 786440 | tf_op jit(solution)/shard_map/ppermute | solution.py:187
  91.9 38.6 %collective-permute-start.4 = (f32[2,256,128]{2,1,0:T(8,128)}, f32[2,256,128]{2,1,0:T(8,128)S(1)}, u32[]{:S(2)}, u32[]{:S(2)}) collective-permute-start(f32[2,256,128]{2,1,0:T(8,128)} %get-tuple-element.38), channel_id=1, source_target_pairs={{0,48},{16,64},{32,80},{48,96},{64,112},{80,0},{96,16},{112,32},{1... | collective-permute-start | bytes 786440 | tf_op jit(solution)/shard_map/ppermute | solution.py:187
  98.7 35.8 %collective-permute-start.5 = (f32[2,256,128]{2,1,0:T(8,128)}, f32[2,256,128]{2,1,0:T(8,128)}, u32[]{:S(2)}, u32[]{:S(2)}) collective-permute-start(f32[2,256,128]{2,1,0:T(8,128)} %get-tuple-element.39), channel_id=1, source_target_pairs={{0,32},{16,48},{32,64},{48,80},{64,96},{80,112},{96,0},{112,16},{1... | collective-permute-start | bytes 786440 | tf_op jit(solution)/shard_map/ppermute | solution.py:187
  111.5 26.6 %collective-permute-start.6 = (f32[2,256,128]{2,1,0:T(8,128)}, f32[2,256,128]{2,1,0:T(8,128)}, u32[]{:S(2)}, u32[]{:S(2)}) collective-permute-start(f32[2,256,128]{2,1,0:T(8,128)} %get-tuple-element.40), channel_id=1, source_target_pairs={{0,16},{16,32},{32,48},{48,64},{64,80},{80,96},{96,112},{112,0},{1... | collective-permute-start | bytes 786440 | tf_op jit(solution)/shard_map/ppermute | solution.py:187
  188.2 121.7 %all-to-all-start.2 = ((f32[8,256,128]{2,1,0:T(8,128)}), f32[8,256,128]{2,1,0:T(8,128)S(1)}, u32[]{:S(2)}, u32[]{:S(2)}) async-start(f32[8,256,128]{2,1,0:T(8,128)} %get-tuple-element.59), calls=%async_computation.2 | async-start | bytes 2097152 | tf_op jit(solution)/shard_map/all_to_all | solution.py:458
  195.6 25.8 %collective-permute-start.8 = (f32[1,256,128]{2,1,0:T(8,128)}, f32[1,256,128]{2,1,0:T(8,128)S(1)}, u32[]{:S(2)}, u32[]{:S(2)}) collective-permute-start(f32[1,256,128]{2,1,0:T(8,128)} %get-tuple-element.43), channel_id=1, source_target_pairs={{0,112},{16,0},{32,16},{48,32},{64,48},{80,64},{96,80},{112,96},{1... | collective-permute-start | bytes 393224 | tf_op jit(solution)/shard_map/ppermute | solution.py:187
  198.8 31.2 %collective-permute-start.9 = (f32[1,256,128]{2,1,0:T(8,128)}, f32[1,256,128]{2,1,0:T(8,128)S(1)}, u32[]{:S(2)}, u32[]{:S(2)}) collective-permute-start(f32[1,256,128]{2,1,0:T(8,128)} %get-tuple-element.44), channel_id=1, source_target_pairs={{0,96},{16,112},{32,0},{48,16},{64,32},{80,48},{96,64},{112,80},{1... | collective-permute-start | bytes 393224 | tf_op jit(solution)/shard_map/ppermute | solution.py:187
  201.1 34.7 %collective-permute-start.10 = (f32[1,256,128]{2,1,0:T(8,128)}, f32[1,256,128]{2,1,0:T(8,128)S(1)}, u32[]{:S(2)}, u32[]{:S(2)}) collective-permute-start(f32[1,256,128]{2,1,0:T(8,128)} %get-tuple-element.45), channel_id=1, source_target_pairs={{0,80},{16,96},{32,112},{48,0},{64,16},{80,32},{96,48},{112,64},{1... | collective-permute-start | bytes 393224 | tf_op jit(solution)/shard_map/ppermute | solution.py:187
  202.5 33.3 %collective-permute-start.11 = (f32[1,256,128]{2,1,0:T(8,128)}, f32[1,256,128]{2,1,0:T(8,128)}, u32[]{:S(2)}, u32[]{:S(2)}) collective-permute-start(f32[1,256,128]{2,1,0:T(8,128)} %get-tuple-element.46), channel_id=1, source_target_pairs={{0,64},{16,80},{32,96},{48,112},{64,0},{80,16},{96,32},{112,48},{1... | collective-permute-start | bytes 393224 | tf_op jit(solution)/shard_map/ppermute | solution.py:187
  206.1 29.7 %collective-permute-start.12 = (f32[1,256,128]{2,1,0:T(8,128)}, f32[1,256,128]{2,1,0:T(8,128)}, u32[]{:S(2)}, u32[]{:S(2)}) collective-permute-start(f32[1,256,128]{2,1,0:T(8,128)} %get-tuple-element.47), channel_id=1, source_target_pairs={{0,48},{16,64},{32,80},{48,96},{64,112},{80,0},{96,16},{112,32},{1... | collective-permute-start | bytes 393224 | tf_op jit(solution)/shard_map/ppermute | solution.py:187
  221.4 18.0 %collective-permute-start.13 = (f32[1,256,128]{2,1,0:T(8,128)}, f32[1,256,128]{2,1,0:T(8,128)}, u32[]{:S(2)}, u32[]{:S(2)}) collective-permute-start(f32[1,256,128]{2,1,0:T(8,128)} %get-tuple-element.48), channel_id=1, source_target_pairs={{0,32},{16,48},{32,64},{48,80},{64,96},{80,112},{96,0},{112,16},{1... | collective-permute-start | bytes 393224 | tf_op jit(solution)/shard_map/ppermute | solution.py:187
  230.0 10.9 %collective-permute-start.14 = (f32[1,256,128]{2,1,0:T(8,128)}, f32[1,256,128]{2,1,0:T(8,128)}, u32[]{:S(2)}, u32[]{:S(2)}) collective-permute-start(f32[1,256,128]{2,1,0:T(8,128)} %get-tuple-element.49), channel_id=1, source_target_pairs={{0,16},{16,32},{32,48},{48,64},{64,80},{80,96},{96,112},{112,0},{1... | collective-permute-start | bytes 393224 | tf_op jit(solution)/shard_map/ppermute | solution.py:187
  252.5 12.2 %collective-permute-start.15 = (f32[1,256,128]{2,1,0:T(8,128)}, f32[1,256,128]{2,1,0:T(8,128)S(1)}, u32[]{:S(2)}, u32[]{:S(2)}) collective-permute-start(f32[1,256,128]{2,1,0:T(8,128)} %get-tuple-element.51), channel_id=1, source_target_pairs={{0,112},{16,0},{32,16},{48,32},{64,48},{80,64},{96,80},{112,96},{1... | collective-permute-start | bytes 393224 | tf_op jit(solution)/shard_map/ppermute | solution.py:187
  254.1 18.2 %collective-permute-start.16 = (f32[1,256,128]{2,1,0:T(8,128)}, f32[1,256,128]{2,1,0:T(8,128)S(1)}, u32[]{:S(2)}, u32[]{:S(2)}) collective-permute-start(f32[1,256,128]{2,1,0:T(8,128)} %get-tuple-element.52), channel_id=1, source_target_pairs={{0,96},{16,112},{32,0},{48,16},{64,32},{80,48},{96,64},{112,80},{1... | collective-permute-start | bytes 393224 | tf_op jit(solution)/shard_map/ppermute | solution.py:187
  256.4 18.2 %collective-permute-start.17 = (f32[1,256,128]{2,1,0:T(8,128)}, f32[1,256,128]{2,1,0:T(8,128)S(1)}, u32[]{:S(2)}, u32[]{:S(2)}) collective-permute-start(f32[1,256,128]{2,1,0:T(8,128)} %get-tuple-element.53), channel_id=1, source_target_pairs={{0,80},{16,96},{32,112},{48,0},{64,16},{80,32},{96,48},{112,64},{1... | collective-permute-start | bytes 393224 | tf_op jit(solution)/shard_map/ppermute | solution.py:187
  257.6 17.1 %collective-permute-start.18 = (f32[1,256,128]{2,1,0:T(8,128)}, f32[1,256,128]{2,1,0:T(8,128)S(1)}, u32[]{:S(2)}, u32[]{:S(2)}) collective-permute-start(f32[1,256,128]{2,1,0:T(8,128)} %get-tuple-element.54), channel_id=1, source_target_pairs={{0,64},{16,80},{32,96},{48,112},{64,0},{80,16},{96,32},{112,48},{1... | collective-permute-start | bytes 393224 | tf_op jit(solution)/shard_map/ppermute | solution.py:187
  261.4 18.6 %collective-permute-start.19 = (f32[1,256,128]{2,1,0:T(8,128)}, f32[1,256,128]{2,1,0:T(8,128)S(1)}, u32[]{:S(2)}, u32[]{:S(2)}) collective-permute-start(f32[1,256,128]{2,1,0:T(8,128)} %get-tuple-element.55), channel_id=1, source_target_pairs={{0,48},{16,64},{32,80},{48,96},{64,112},{80,0},{96,16},{112,32},{1... | collective-permute-start | bytes 393224 | tf_op jit(solution)/shard_map/ppermute | solution.py:187
  264.7 16.5 %collective-permute-start.20 = (f32[1,256,128]{2,1,0:T(8,128)}, f32[1,256,128]{2,1,0:T(8,128)S(1)}, u32[]{:S(2)}, u32[]{:S(2)}) collective-permute-start(f32[1,256,128]{2,1,0:T(8,128)} %get-tuple-element.56), channel_id=1, source_target_pairs={{0,32},{16,48},{32,64},{48,80},{64,96},{80,112},{96,0},{112,16},{1... | collective-permute-start | bytes 393224 | tf_op jit(solution)/shard_map/ppermute | solution.py:187
  272.2 12.9 %collective-permute-start.21 = (f32[1,256,128]{2,1,0:T(8,128)}, f32[1,256,128]{2,1,0:T(8,128)S(1)}, u32[]{:S(2)}, u32[]{:S(2)}) collective-permute-start(f32[1,256,128]{2,1,0:T(8,128)} %get-tuple-element.57), channel_id=1, source_target_pairs={{0,16},{16,32},{32,48},{48,64},{64,80},{80,96},{96,112},{112,0},{1... | collective-permute-start | bytes 393224 | tf_op jit(solution)/shard_map/ppermute | solution.py:187
  293.4 5.3 %collective-permute-start.23 = (f32[8,128]{1,0:T(8,128)}, f32[8,128]{1,0:T(8,128)S(1)}, u32[]{:S(2)}, u32[]{:S(2)}) collective-permute-start(f32[8,128]{1,0:T(8,128)} %get-tuple-element.62), channel_id=1, source_target_pairs={{0,2},{1,3},{2,0},{3,1},{4,6},{5,7},{6,4},{7,5},{8,10},{9,11},{10,... | collective-permute-start | bytes 12296 | tf_op jit(solution)/shard_map/ppermute | solution.py:480
  307.8 7.1 %collective-permute-start.30 = (f32[8,128]{1,0:T(8,128)S(1)}, f32[8,128]{1,0:T(8,128)S(1)}, u32[]{:S(2)}, u32[]{:S(2)}) collective-permute-start(f32[8,128]{1,0:T(8,128)S(1)} %add_add_fusion.2), channel_id=1, source_target_pairs={{0,16},{16,0},{32,48},{48,32},{64,80},{80,64},{96,112},{112,96},{1... | collective-permute-start | bytes 12296 | tf_op jit(solution)/shard_map/ppermute | solution.py:480
  308.8 6.1 %collective-permute-start.31 = (f32[8,128]{1,0:T(8,128)S(1)}, f32[8,128]{1,0:T(8,128)S(1)}, u32[]{:S(2)}, u32[]{:S(2)}) collective-permute-start(f32[8,128]{1,0:T(8,128)S(1)} %add_add_fusion.2), channel_id=1, source_target_pairs={{0,144},{16,128},{32,176},{48,160},{64,208},{80,192},{96,240},{112... | collective-permute-start | bytes 12296 | tf_op jit(solution)/shard_map/ppermute | solution.py:480
  308.8 6.1 %collective-permute-start.29 = (f32[8,128]{1,0:T(8,128)S(1)}, f32[8,128]{1,0:T(8,128)S(1)}, u32[]{:S(2)}, u32[]{:S(2)}) collective-permute-start(f32[8,128]{1,0:T(8,128)S(1)} %add_add_fusion.2), channel_id=1, source_target_pairs={{0,128},{16,144},{32,160},{48,176},{64,192},{80,208},{96,224},{112... | collective-permute-start | bytes 12296 | tf_op jit(solution)/shard_map/ppermute | solution.py:480
  314.9 8.0 %collective-permute-start.22 = (f32[16,128]{1,0:T(8,128)}, f32[16,128]{1,0:T(8,128)S(1)}, u32[]{:S(2)}, u32[]{:S(2)}) collective-permute-start(f32[16,128]{1,0:T(8,128)} %get-tuple-element.61), channel_id=1, source_target_pairs={{0,128},{128,0},{1,129},{129,1},{2,130},{130,2},{3,131},{131,3},{4... | collective-permute-start | bytes 24584 | tf_op jit(solution)/shard_map/ppermute | solution.py:474
  314.9 9.3 %collective-permute-start.33 = (f32[8,128]{1,0:T(8,128)S(1)}, f32[8,128]{1,0:T(8,128)S(1)}, u32[]{:S(2)}, u32[]{:S(2)}) collective-permute-start(f32[8,128]{1,0:T(8,128)S(1)} %add_add_fusion.1), channel_id=1, source_target_pairs={{0,32},{16,48},{32,64},{48,80},{64,96},{80,112},{96,0},{112,16},{1... | collective-permute-start | bytes 12296 | tf_op jit(solution)/shard_map/ppermute | solution.py:480
  315.9 8.3 %collective-permute-start.34 = (f32[8,128]{1,0:T(8,128)S(1)}, f32[8,128]{1,0:T(8,128)S(1)}, u32[]{:S(2)}, u32[]{:S(2)}) collective-permute-start(f32[8,128]{1,0:T(8,128)S(1)} %add_add_fusion.1), channel_id=1, source_target_pairs={{0,96},{16,112},{32,0},{48,16},{64,32},{80,48},{96,64},{112,80},{1... | collective-permute-start | bytes 12296 | tf_op jit(solution)/shard_map/ppermute | solution.py:480
  319.1 7.5 %collective-permute-start.32 = (f32[8,128]{1,0:T(8,128)S(1)}, f32[8,128]{1,0:T(8,128)S(1)}, u32[]{:S(2)}, u32[]{:S(2)}) collective-permute-start(f32[8,128]{1,0:T(8,128)S(1)} %add_add_fusion.1), channel_id=1, source_target_pairs={{0,64},{16,80},{32,96},{48,112},{64,0},{80,16},{96,32},{112,48},{1... | collective-permute-start | bytes 12296 | tf_op jit(solution)/shard_map/ppermute | solution.py:480
  (25 other events, 280.9 us)
